TPU v7x, 32 devices: a whole 2x2x4 slice. The times are simulated.
32 devices in a mesh: groups: 2 (over y), sub: 16 (over z, x, core).
Axes of the slice: x: 2, y: 2, z: 4, core: 2. Of those that a mesh axis runs over, the one named last changes fastest.
Arguments:
- samples: bfloat16 [16896, 512], P(('groups', 'sub')), parts along dimension 0, may hold values from -6 to 6
- channel_order: int32 [512], replicated, may hold values from 0 to 511, each once
- merge_table: int32 [9, 3, 256], replicated, may hold values from 0 to 128, as said below
Outputs:
- spectra: float32 [512, 4096], P(('groups', 'sub')), parts along dimension 0
There are 2 independent parts, one for each index of `groups`. A program takes and returns all parts, laid end to end along the dimension named above; an argument that names none is the same for every part. Nothing has to cross between parts.
Inputs may be any that keep to these rules, and one draw needn't show every extreme that they name: `channel_order`: a permutation of the 512 channels. `merge_table`: for level l, entry j is row d = j % 2**(l-1) of merged subband j // 2**(l-1); with C = max(1, 2**(l-2)) and e = 8, entries 0 and 1 lie in [e * (d // (2 e)), e * (d // (2 e)) + min(C, e)), and entry 2 equals entry 0 or entry 0 plus 1.
All inputs are finite; a program needn't handle non-finite values.
Results may differ from a plain program's by a relative error of at most 0.012.
Values may be sent and summed in bfloat16 or wider, within the bound.
A program may use at most 64 MiB of HBM per device.

v0:
```python
import functools
import math

import jax
import jax.numpy as jnp
from jax import lax
from jax.experimental import pallas as pl
from jax.experimental.pallas import tpu as pltpu
from jax.sharding import PartitionSpec as P

LOCAL = 5
MESH = pl.DeviceIdType.MESH
CH_DEV = 32
SAMPLES = 8192


def from_partner(block, axis, apart):
    count = lax.axis_size(axis)
    route = []
    for low in range(count):
        high = low | 1 << apart
        if high != low and high < count:
            route += [(low, high), (high, low)]
    return lax.ppermute(block, axis, route)


def delay_rows(values, shifts, margin, time_axis):
    length = values.shape[time_axis]
    moved = values
    for bit_num in range(max(1, margin.bit_length())):
        offset = 2**bit_num
        rolled = jnp.pad(moved[:, offset:], ((0, 0), (0, offset)))
        flagged = shifts >> bit_num & 1 == 1
        flagged = flagged[:, None]
        moved = jnp.where(flagged, rolled, moved)
    return moved


def merge_level(current, entries, child_rows, span_rows, time_axis):
    outputs = jnp.arange(entries.shape[1], dtype=jnp.int32)
    starts = 2 * child_rows * (outputs // span_rows)
    lower_rows = jnp.take(current, starts + entries[0], axis=1 - time_axis)
    upper_rows = jnp.take(current, starts + child_rows + entries[1], axis=1 - time_axis)
    moved_rows = delay_rows(upper_rows, entries[2], child_rows, time_axis)
    return (lower_rows.astype(jnp.float32) + moved_rows.astype(jnp.float32)).astype(jnp.bfloat16)


def spectrum(delays, channels):
    row_count = delays.shape[0]
    length = delays.shape[1]
    fold_size = length // 128
    first_index = jnp.arange(fold_size, dtype=jnp.int32)
    lane_index = jnp.arange(128, dtype=jnp.int32)
    half_index = jnp.arange(64, dtype=jnp.int32)
    angle_one = (
        2.0
        * math.pi
        / fold_size
        * (first_index[:, None] * first_index[None, :] % fold_size).astype(jnp.float32)
    )
    cos_one = jnp.cos(angle_one).astype(jnp.bfloat16)
    sin_one = jnp.sin(angle_one).astype(jnp.bfloat16)
    angle_two = (
        2.0
        * math.pi
        / length
        * (first_index[:, None] * lane_index[None, :] % length).astype(jnp.float32)
    )
    twist_cos = jnp.cos(angle_two)
    twist_sin = jnp.sin(angle_two)
    angle_three = (
        2.0 * math.pi / 128 * (lane_index[:, None] * half_index[None, :] % 128).astype(jnp.float32)
    )
    cos_three = jnp.cos(angle_three).astype(jnp.bfloat16)
    sin_three = jnp.sin(angle_three).astype(jnp.bfloat16)
    series = delays.reshape(row_count, fold_size, 128)
    first_re = jnp.einsum("kn,rnm->rkm", cos_one, series, preferred_element_type=jnp.float32)
    first_im = -jnp.einsum("kn,rnm->rkm", sin_one, series, preferred_element_type=jnp.float32)
    twisted_re = (first_re * twist_cos + first_im * twist_sin).astype(jnp.bfloat16)
    twisted_im = (first_im * twist_cos - first_re * twist_sin).astype(jnp.bfloat16)
    out_re = jnp.einsum(
        "rkn,nj->rjk", twisted_re, cos_three, preferred_element_type=jnp.float32
    ) + jnp.einsum("rkn,nj->rjk", twisted_im, sin_three, preferred_element_type=jnp.float32)
    out_im = jnp.einsum(
        "rkn,nj->rjk", twisted_im, cos_three, preferred_element_type=jnp.float32
    ) - jnp.einsum("rkn,nj->rjk", twisted_re, sin_three, preferred_element_type=jnp.float32)
    power = (out_re * out_re + out_im * out_im) / (length * channels)
    return power.reshape(row_count, 64 * fold_size)


def local(samples, channel_order, merge_table):
    owners = lax.axis_size("sub")
    owner_index = lax.axis_index("sub")
    owned_rows = CH_DEV // 2
    quarter = CH_DEV // 4
    window = samples.shape[0]
    channels = samples.shape[1]
    ordered = jnp.take(samples, channel_order, axis=1).T.reshape(owners, CH_DEV, window)
    current = lax.all_to_all(ordered, "sub", split_axis=0, concat_axis=2, tiled=True).reshape(
        CH_DEV, window * owners
    )
    for level_num in range(1, LOCAL + 1):
        entries = lax.dynamic_slice_in_dim(
            merge_table[level_num - 1], owner_index * owned_rows, owned_rows, 1
        )
        current = merge_level(
            current, entries, max(1, 2 ** (level_num - 2)), 2 ** (level_num - 1), 1
        )
    block_index = jnp.zeros((), jnp.int32)
    for bit_num in range(owners.bit_length() - 1):
        level_num = LOCAL + bit_num + 1
        half_bit = owner_index >> bit_num & 1
        block_index = block_index * 2 + half_bit
        span_rows = owned_rows * 2 ** (bit_num + 1)
        child_rows = span_rows // 2
        subband = owner_index >> bit_num + 1
        entries = lax.dynamic_slice_in_dim(
            merge_table[level_num - 1],
            subband * span_rows + owned_rows * block_index,
            owned_rows,
            1,
        )
        kept_rows = lax.dynamic_slice_in_dim(current, half_bit * quarter, quarter, 0)
        sent_rows = lax.dynamic_slice_in_dim(current, (1 - half_bit) * quarter, quarter, 0)
        partner = from_partner(sent_rows, "sub", bit_num)
        row_base = quarter * block_index
        is_low = half_bit == 0
        lower_part = jnp.where(is_low, kept_rows, partner)
        upper_part = jnp.where(is_low, partner, kept_rows)
        lower_rows = jnp.take(lower_part, entries[0] - row_base, axis=0)
        upper_rows = jnp.take(upper_part, entries[1] - row_base, axis=0)
        moved_rows = delay_rows(upper_rows, entries[2], child_rows, 1)
        current = (lower_rows.astype(jnp.float32) + moved_rows.astype(jnp.float32)).astype(
            jnp.bfloat16
        )
    return spectrum(current[:, :SAMPLES], channels)


def reversed_bits(values, bits):
    flipped = jnp.zeros_like(values)
    for bit_num in range(bits):
        flipped = flipped | ((values >> bit_num & 1) << (bits - 1 - bit_num))
    return flipped


def one_hot(row_index, depth):
    rows = lax.broadcasted_iota(jnp.int32, (depth, row_index.shape[1]), 0)
    return (rows == row_index).astype(jnp.float32).astype(jnp.bfloat16)


def merge_kernel(
    owners,
    step,
    order_hbm,
    table_hbm,
    own_ref,
    out_ref,
    order_ref,
    table_ref,
    joined,
    current,
    picks,
    first_pick,
    turned,
    halo_send,
    halo_recv,
    block_send,
    block_recv,
    load_sem,
):
    levels, _, rows = table_ref.shape
    extra = step * (owners - 1)
    window = own_ref.shape[0]
    _, held, length = out_ref.shape
    whole = length + rows
    me = lax.axis_index("sub")

    loads = [
        pltpu.make_async_copy(order_hbm, order_ref, load_sem.at[0]),
        pltpu.make_async_copy(table_hbm, table_ref, load_sem.at[1]),
        pltpu.make_async_copy(own_ref, joined.at[extra : extra + window], load_sem.at[2]),
    ]
    for load in loads:
        load.start()
    barrier = pltpu.get_barrier_semaphore()
    for apart in range(1, owners):
        pl.semaphore_signal(
            barrier, inc=1, device_id={"sub": lax.rem(me + apart, owners)}, device_id_type=MESH
        )
    loads[0].wait()
    channels = order_ref.shape[1]
    column = lax.broadcasted_iota(jnp.int32, (1, channels), 1)
    split = jnp.where(column < rows, 2 * column, 2 * (column - rows) + 1)
    first_pick[...] = jnp.dot(
        one_hot(order_ref[...], channels),
        one_hot(split, channels),
        preferred_element_type=jnp.float32,
    ).astype(jnp.bfloat16)
    pl.semaphore_wait(barrier, owners - 1)

    onward = pltpu.make_async_remote_copy(
        src_ref=own_ref.at[window - extra :],
        dst_ref=joined.at[0:extra],
        send_sem=halo_send.at[0],
        recv_sem=halo_recv.at[0],
        device_id={"sub": lax.rem(me + 1, owners)},
        device_id_type=MESH,
    )
    back = pltpu.make_async_remote_copy(
        src_ref=own_ref.at[0:extra],
        dst_ref=joined.at[extra + window :],
        send_sem=halo_send.at[1],
        recv_sem=halo_recv.at[1],
        device_id={"sub": lax.rem(me + owners - 1, owners)},
        device_id_type=MESH,
    )

    @pl.when(me < owners - 1)
    def _():
        onward.start()

    @pl.when(me > 0)
    def _():
        back.start()

    loads[1].wait()
    lanes = lax.broadcasted_iota(jnp.int32, (1, rows), 1)
    for level_num in range(2, levels + 1):
        child_rows = max(1, 2 ** (level_num - 2))
        entries = table_ref[level_num - 1]
        starts = 2 * child_rows * (lanes >> (level_num - 1))
        picks[level_num - 2, :, 0:rows] = one_hot(starts + entries[0:1], rows)
        picks[level_num - 2, :, rows:] = one_hot(starts + child_rows + entries[1:2], rows)

    @pl.when(me < owners - 1)
    def _():
        onward.wait_send()
        back.wait_recv()

    @pl.when(me > 0)
    def _():
        back.wait_send()
        onward.wait_recv()

    loads[2].wait()
    first = pl.multiple_of(extra - step * me, step)
    have = whole
    left = rows
    for level_num in range(1, levels + 1):
        child_rows = max(1, 2 ** (level_num - 2))
        shifts = table_ref[level_num - 1][2:3]
        if level_num == 1:
            chosen = first_pick[...]
            source = joined[pl.ds(first, whole), :]
        else:
            chosen = picks[level_num - 2]
            source = current[0:have, :]
        left -= child_rows
        keep = -(-(length + left) // 16) * 16
        picked = jnp.dot(source, chosen, preferred_element_type=jnp.float32)
        for base in range(0, rows, 128):
            moved = picked[:, rows + base : rows + base + 128]
            amounts = shifts[:, base : base + 128]
            for bit_num in reversed(range(child_rows.bit_length())):
                size = moved.shape[0]
                rolled = pltpu.roll(moved, size - 2**bit_num, axis=0)
                flagged = jnp.broadcast_to(amounts >> bit_num & 1, moved.shape) == 1
                moved = jnp.where(flagged, rolled, moved)
                needed = min(size, keep + -(-(2**bit_num - 1) // 8) * 8)
                moved = moved[0:needed]
            current[0:keep, base : base + 128] = (
                picked[0:keep, base : base + 128] + moved[0:keep]
            ).astype(jnp.bfloat16)
        have = keep
    places = lax.broadcasted_iota(jnp.int32, (rows, rows), 0)
    shift = held.bit_length() - 1
    sources = (reversed_bits(places >> shift, owners.bit_length() - 1) << shift) + (places & (held - 1))
    placed = (lax.broadcasted_iota(jnp.int32, (rows, rows), 1) == sources).astype(jnp.float32)
    turned[...] = lax.dot_general(
        placed.astype(jnp.bfloat16),
        current[0:length, :],
        (((1,), (1,)), ((), ())),
        preferred_element_type=jnp.float32,
    ).astype(jnp.bfloat16)

    copies = []
    for apart in range(1, owners):
        target = lax.rem(me + apart, owners)
        copy = pltpu.make_async_remote_copy(
            src_ref=turned.at[pl.ds(pl.multiple_of(target * held, held), held)],
            dst_ref=out_ref.at[me],
            send_sem=block_send.at[apart],
            recv_sem=block_recv.at[apart],
            device_id={"sub": target},
            device_id_type=MESH,
        )
        copy.start()
        copies.append(copy)
    out_ref[me] = turned[pl.ds(pl.multiple_of(me * held, held), held), :]
    for copy in copies:
        copy.wait()


def local_sliced(samples, channel_order, merge_table):
    owners = lax.axis_size("sub")
    window, channels = samples.shape
    levels, _, rows = merge_table.shape
    held = rows // owners
    length = window - held
    step = window - length
    extra = step * (owners - 1)
    order = channel_order.reshape(1, channels)
    vmem = pl.BlockSpec(memory_space=pltpu.VMEM)
    blocks = pl.pallas_call(
        functools.partial(merge_kernel, owners, step),
        out_shape=jax.ShapeDtypeStruct((owners, held, length), jnp.bfloat16),
        in_specs=[pl.BlockSpec(memory_space=pl.ANY)] * 3,
        out_specs=vmem,
        scratch_shapes=[
            pltpu.VMEM((1, channels), jnp.int32),
            pltpu.VMEM((levels, 3, rows), jnp.int32),
            pltpu.VMEM((window + 2 * extra, channels), jnp.bfloat16),
            pltpu.VMEM((length + rows, rows), jnp.bfloat16),
            pltpu.VMEM((levels - 1, rows, 2 * rows), jnp.bfloat16),
            pltpu.VMEM((channels, channels), jnp.bfloat16),
            pltpu.VMEM((rows, length), jnp.bfloat16),
            pltpu.SemaphoreType.DMA((2,)),
            pltpu.SemaphoreType.DMA((2,)),
            pltpu.SemaphoreType.DMA((owners,)),
            pltpu.SemaphoreType.DMA((owners,)),
            pltpu.SemaphoreType.DMA((3,)),
        ],
        compiler_params=pltpu.CompilerParams(
            vmem_limit_bytes=62 * 1024 * 1024, collective_id=0, has_side_effects=True
        ),
        name="merge_rows",
    )(order, merge_table, samples)
    series = blocks.transpose(1, 0, 2).reshape(held, owners * length)
    return spectrum(series, channels)


def is_sliced(window, owners, rows):
    step = rows // owners
    length = window - step
    return step % 16 == 0 and length % 128 == 0 and step * (owners - 1) <= window


def local_any(samples, channel_order, merge_table):
    if is_sliced(samples.shape[0], lax.axis_size("sub"), merge_table.shape[2]):
        return local_sliced(samples, channel_order, merge_table)
    return local(samples, channel_order, merge_table)


def solution(mesh):
    in_specs = (P(("groups", "sub"), None), P(), P())
    out_specs = P(("groups", "sub"), None)
    return jax.shard_map(local_any, mesh=mesh, in_specs=in_specs, out_specs=out_specs, check_vma=False)
```

profile of v0, /device:TPU:0, one launch (start us, length us, event | category | flops | bytes accessed | tf_op | source)
XLA Modules:
  0.0 26.7 jit_solution(5361278260538686356)
XLA Ops:
  0.0 0.1 fusion.30
  0.1 21.9 %merge_rows.1 = bf16[16,16,512]{2,1,0:T(8,128)(2,1)} custom-call(s32[1,512]{1,0:T(1,128)} %bitcast.31, s32[9,3,256]{2,1,0:T(4,128)} %table_hbm.1, bf16[528,512]{1,0:T(8,128)(2,1)} %own_ref.1), custom_call_target="tpu_custom_call" | custom-call | tf_op jit(solution)/shard_map/merge_rows/pallas_call | solution.py:314
  22.1 1.1 %copy.4 = bf16[16,16,512]{2,1,0:T(8,128)(2,1)S(1)} copy(bf16[16,16,512]{2,0,1:T(8,128)(2,1)} %bitcast.30) | data formatting | bytes 524288 | tf_op jit(solution)/shard_map/transpose | solution.py:338
  23.2 0.2 reshape_reshape.3
  23.4 0.3 %convolution_bitcast_fusion = f32[16,64,128]{2,1,0:T(8,128)S(1)} fusion(bf16[16,64,128]{2,1,0:T(8,128)(2,1)S(1)} %reshape_reshape.3), kind=kOutput, calls=%fused_computation.2 | convolution fusion | flops 16838656 | bytes 786432 | tf_op jit(solution)/shard_map/kn,rnm->rkm/dot_general | solution.py:77
  23.7 0.4 %add_convert_fusion = (bf16[16,64,128]{2,1,0:T(8,128)(2,1)S(1)}, bf16[16,64,128]{2,1,0:T(8,128)(2,1)S(1)}) fusion(f32[16,64,128]{2,1,0:T(8,128)S(1)} %convolution_bitcast_fusion, f32[64,128]{1,0:T(8,128)S(1)} %get-tuple-element.7, f32[64,128]{1,0:T(8,128)S(1)} %get-tuple-element.8, bf16[16,64,128]{2,1,0:T(8,128)(2,1)S(1)} %reshape_reshape.3), kind=kOutput, calls=%fused_computation.11 | convolution fusion | flops 18018304 | bytes 1376256 | tf_op jit(solution)/shard_map/kn,rnm->rkm/dot_general | solution.py:78
  24.1 0.4 %fusion.38 = f32[64,16,64]{2,0,1:T(8,128)S(1)} fusion(bf16[16,64,128]{2,1,0:T(8,128)(2,1)S(1)} %get-tuple-element.5), kind=kOutput, calls=%fused_computation.50 | convolution fusion | flops 16900096 | bytes 524288 | tf_op jit(solution)/shard_map/rkn,nj->rjk/dot_general | solution.py:81
  24.5 0.4 %fusion.36 = f32[64,16,64]{2,0,1:T(8,128)S(1)} fusion(bf16[16,64,128]{2,1,0:T(8,128)(2,1)S(1)} %get-tuple-element.6), kind=kOutput, calls=%fused_computation.49 | convolution fusion | flops 16900096 | bytes 524288 | tf_op jit(solution)/shard_map/rkn,nj->rjk/dot_general | solution.py:84
  24.9 0.4 %fusion.1 = f32[64,16,64]{2,0,1:T(8,128)S(1)} fusion(f32[64,16,64]{2,0,1:T(8,128)S(1)} %fusion.36, bf16[16,64,128]{2,1,0:T(8,128)(2,1)S(1)} %get-tuple-element.5), kind=kOutput, calls=%fused_computation.4 | convolution fusion | flops 17031168 | bytes 786432 | tf_op jit(solution)/shard_map/rkn,nj->rjk/dot_general | solution.py:86
  25.3 0.4 %fusion.5 = f32[16,64,64]{2,1,0:T(8,128)S(1)} fusion(f32[64,16,64]{2,0,1:T(8,128)S(1)} %fusion.1, f32[64,16,64]{2,0,1:T(8,128)S(1)} %fusion.38, bf16[16,64,128]{2,1,0:T(8,128)(2,1)S(1)} %get-tuple-element.6), kind=kOutput, calls=%fused_computation.9 | convolution fusion | flops 17162240 | bytes 1048576 | tf_op jit(solution)/shard_map/rkn,nj->rjk/dot_general | solution.py:83
  25.8 0.9 %reshape.43 = f32[16,4096]{1,0:T(8,128)} reshape(f32[16,64,64]{2,1,0:T(8,128)S(1)} %fusion.5) | data formatting | bytes 524288 | tf_op jit(solution)/shard_map/reshape | solution.py:88
where the time goes:
time: 26.8 us; the launch traced here: 26.7 us
  Pallas kernels  21.9 us (82%)
  matrix products  2.38 us (9%)
  local copies, waits for them, and re-layouts  2.16 us (8%)
    pallas_call x1, Pallas kernels, local_sliced(): pl.pallas_call(functools.partial(merge_kernel, owners, step), out_shape=j...  21.9 us
    transpose x1, local copies, waits for them, and re-layouts, local_sliced(): series = blocks.transpose(1, 0, 2).reshape(held, owners * length)  1.1 us
    reshape x1, local copies, waits for them, and re-layouts, spectrum(): return power.reshape(row_count, 64 * fold_size)  0.89 us

commit v1 on v0

v1 whole, which is shorter than its diff:
```python
import functools
import math

import jax
import jax.numpy as jnp
import numpy as np
from jax import lax
from jax.experimental import pallas as pl
from jax.experimental.pallas import tpu as pltpu
from jax.sharding import PartitionSpec as P

LOCAL = 5
MESH = pl.DeviceIdType.MESH
CH_DEV = 32
SAMPLES = 8192


def from_partner(block, axis, apart):
    count = lax.axis_size(axis)
    route = []
    for low in range(count):
        high = low | 1 << apart
        if high != low and high < count:
            route += [(low, high), (high, low)]
    return lax.ppermute(block, axis, route)


def delay_rows(values, shifts, margin, time_axis):
    length = values.shape[time_axis]
    moved = values
    for bit_num in range(max(1, margin.bit_length())):
        offset = 2**bit_num
        rolled = jnp.pad(moved[:, offset:], ((0, 0), (0, offset)))
        flagged = shifts >> bit_num & 1 == 1
        flagged = flagged[:, None]
        moved = jnp.where(flagged, rolled, moved)
    return moved


def merge_level(current, entries, child_rows, span_rows, time_axis):
    outputs = jnp.arange(entries.shape[1], dtype=jnp.int32)
    starts = 2 * child_rows * (outputs // span_rows)
    lower_rows = jnp.take(current, starts + entries[0], axis=1 - time_axis)
    upper_rows = jnp.take(current, starts + child_rows + entries[1], axis=1 - time_axis)
    moved_rows = delay_rows(upper_rows, entries[2], child_rows, time_axis)
    return (lower_rows.astype(jnp.float32) + moved_rows.astype(jnp.float32)).astype(jnp.bfloat16)


def spectrum(delays, channels):
    row_count = delays.shape[0]
    length = delays.shape[1]
    fold_size = length // 128
    first_index = jnp.arange(fold_size, dtype=jnp.int32)
    lane_index = jnp.arange(128, dtype=jnp.int32)
    half_index = jnp.arange(64, dtype=jnp.int32)
    angle_one = (
        2.0
        * math.pi
        / fold_size
        * (first_index[:, None] * first_index[None, :] % fold_size).astype(jnp.float32)
    )
    cos_one = jnp.cos(angle_one).astype(jnp.bfloat16)
    sin_one = jnp.sin(angle_one).astype(jnp.bfloat16)
    angle_two = (
        2.0
        * math.pi
        / length
        * (first_index[:, None] * lane_index[None, :] % length).astype(jnp.float32)
    )
    twist_cos = jnp.cos(angle_two)
    twist_sin = jnp.sin(angle_two)
    angle_three = (
        2.0 * math.pi / 128 * (lane_index[:, None] * half_index[None, :] % 128).astype(jnp.float32)
    )
    cos_three = jnp.cos(angle_three).astype(jnp.bfloat16)
    sin_three = jnp.sin(angle_three).astype(jnp.bfloat16)
    series = delays.reshape(row_count, fold_size, 128)
    first_re = jnp.einsum("kn,rnm->rkm", cos_one, series, preferred_element_type=jnp.float32)
    first_im = -jnp.einsum("kn,rnm->rkm", sin_one, series, preferred_element_type=jnp.float32)
    twisted_re = (first_re * twist_cos + first_im * twist_sin).astype(jnp.bfloat16)
    twisted_im = (first_im * twist_cos - first_re * twist_sin).astype(jnp.bfloat16)
    out_re = jnp.einsum(
        "rkn,nj->rjk", twisted_re, cos_three, preferred_element_type=jnp.float32
    ) + jnp.einsum("rkn,nj->rjk", twisted_im, sin_three, preferred_element_type=jnp.float32)
    out_im = jnp.einsum(
        "rkn,nj->rjk", twisted_im, cos_three, preferred_element_type=jnp.float32
    ) - jnp.einsum("rkn,nj->rjk", twisted_re, sin_three, preferred_element_type=jnp.float32)
    power = (out_re * out_re + out_im * out_im) / (length * channels)
    return power.reshape(row_count, 64 * fold_size)


def local(samples, channel_order, merge_table):
    owners = lax.axis_size("sub")
    owner_index = lax.axis_index("sub")
    owned_rows = CH_DEV // 2
    quarter = CH_DEV // 4
    window = samples.shape[0]
    channels = samples.shape[1]
    ordered = jnp.take(samples, channel_order, axis=1).T.reshape(owners, CH_DEV, window)
    current = lax.all_to_all(ordered, "sub", split_axis=0, concat_axis=2, tiled=True).reshape(
        CH_DEV, window * owners
    )
    for level_num in range(1, LOCAL + 1):
        entries = lax.dynamic_slice_in_dim(
            merge_table[level_num - 1], owner_index * owned_rows, owned_rows, 1
        )
        current = merge_level(
            current, entries, max(1, 2 ** (level_num - 2)), 2 ** (level_num - 1), 1
        )
    block_index = jnp.zeros((), jnp.int32)
    for bit_num in range(owners.bit_length() - 1):
        level_num = LOCAL + bit_num + 1
        half_bit = owner_index >> bit_num & 1
        block_index = block_index * 2 + half_bit
        span_rows = owned_rows * 2 ** (bit_num + 1)
        child_rows = span_rows // 2
        subband = owner_index >> bit_num + 1
        entries = lax.dynamic_slice_in_dim(
            merge_table[level_num - 1],
            subband * span_rows + owned_rows * block_index,
            owned_rows,
            1,
        )
        kept_rows = lax.dynamic_slice_in_dim(current, half_bit * quarter, quarter, 0)
        sent_rows = lax.dynamic_slice_in_dim(current, (1 - half_bit) * quarter, quarter, 0)
        partner = from_partner(sent_rows, "sub", bit_num)
        row_base = quarter * block_index
        is_low = half_bit == 0
        lower_part = jnp.where(is_low, kept_rows, partner)
        upper_part = jnp.where(is_low, partner, kept_rows)
        lower_rows = jnp.take(lower_part, entries[0] - row_base, axis=0)
        upper_rows = jnp.take(upper_part, entries[1] - row_base, axis=0)
        moved_rows = delay_rows(upper_rows, entries[2], child_rows, 1)
        current = (lower_rows.astype(jnp.float32) + moved_rows.astype(jnp.float32)).astype(
            jnp.bfloat16
        )
    return spectrum(current[:, :SAMPLES], channels)


LANES = 128
GROUP = 8


def reversed_index(index, bits):
    flipped = 0
    for bit_num in range(bits):
        flipped = flipped * 2 + index // 2**bit_num % 2
    return flipped


def widest_shift(level_num):
    return max(1, 2 ** (level_num - 2))


def still_to_come(level_num, levels):
    return sum(widest_shift(later) for later in range(level_num + 1, levels + 1))


def rounded(values):
    return values.astype(jnp.bfloat16).astype(jnp.float32)


def transform_tables(fold_size, length):
    first_index = np.arange(fold_size)
    lane_index = np.arange(LANES)
    half_index = np.concatenate([np.arange(0, 64, 2), np.arange(1, 64, 2)])
    unit = np.float32(2.0 * math.pi)

    def angles(left, right, period):
        turns = (left[:, None] * right[None, :]) % period
        return (unit / np.float32(period)) * turns.astype(np.float32)

    one = angles(first_index, first_index, fold_size)
    first_table = np.concatenate([np.cos(one), -np.sin(one)], axis=0)
    two = angles(first_index, lane_index, length)
    twist = np.stack([np.cos(two), np.sin(two)])
    three = angles(half_index, lane_index, LANES)
    cos_three, sin_three = np.cos(three), np.sin(three)
    third_table = np.concatenate(
        [
            np.concatenate([cos_three, sin_three], axis=1),
            np.concatenate([-sin_three, cos_three], axis=1),
        ],
        axis=0,
    )
    return (
        jnp.asarray(first_table, jnp.bfloat16),
        jnp.asarray(twist, jnp.float32),
        jnp.asarray(third_table, jnp.bfloat16),
    )


def merge_kernel(
    owners,
    length,
    order_hbm,
    table_hbm,
    own_hbm,
    first_hbm,
    twist_hbm,
    third_hbm,
    out_ref,
    order_ref,
    table_ref,
    own_ref,
    first_ref,
    twist_ref,
    third_ref,
    order_wide,
    table_flat,
    choose,
    lower_at,
    upper_at,
    lane_at,
    picked,
    tables,
    halo_out,
    halo_in,
    early_out,
    late_out,
    early_in,
    late_in,
    folded,
    twisted,
    powers,
    halo_sem,
    early_send,
    early_recv,
    late_send,
    late_recv,
    load_sem,
):
    levels, _, rows = table_ref.shape
    window, channels = own_ref.shape
    held = rows // owners
    pad = -window % LANES
    own_tiles = (window + pad) // LANES
    halo_tiles = rows // LANES
    all_tiles = own_tiles + halo_tiles
    early_tiles = own_tiles - halo_tiles
    fold_size = length // LANES
    turn = window % LANES
    me = lax.axis_index("sub")
    bits = owners.bit_length() - 1

    barrier = pltpu.get_barrier_semaphore()
    for apart in range(1, owners):
        pl.semaphore_signal(
            barrier, inc=1, device_id={"sub": lax.rem(me + apart, owners)}, device_id_type=MESH
        )
    loads = [
        pltpu.make_async_copy(source, target, load_sem.at[place])
        for place, (source, target) in enumerate(
            [
                (order_hbm, order_ref),
                (own_hbm, own_ref),
                (table_hbm, table_ref),
                (first_hbm, first_ref),
                (twist_hbm, twist_ref),
                (third_hbm, third_ref),
            ]
        )
    ]
    for load in loads:
        load.start()

    lane = lax.broadcasted_iota(jnp.int32, (GROUP, LANES), 1)
    lane_rows = lax.broadcasted_iota(jnp.int32, (rows, LANES), 1)

    loads[0].wait()
    order_rows = jnp.broadcast_to(order_ref[...].astype(jnp.float32), (GROUP, channels))
    order_wide[...] = jnp.broadcast_to(order_rows.T[:, 0:1], (channels, LANES))
    lane_float = lane_rows.astype(jnp.float32)
    for half in range(2):
        wanted = order_wide[pl.ds(half, rows, stride=2), :]
        for base in range(0, channels, LANES):
            hit = (wanted == lane_float + float(base)).astype(jnp.float32)
            choose[half * rows : (half + 1) * rows, base : base + LANES] = hit.astype(jnp.bfloat16)

    loads[2].wait()
    table_flat[...] = jnp.zeros_like(table_flat)
    for level_num in range(levels):
        table_flat[3 * level_num : 3 * level_num + 3, :] = table_ref[level_num].astype(jnp.float32)
    turned = table_flat[...].T
    shifted = lane_rows + jnp.broadcast_to(turned[:, 2:3], (rows, LANES)).astype(jnp.int32)
    lane_at[0] = shifted

    def level_one(begin, end):
        size = end - begin
        both = lax.dot_general(
            choose[...],
            own_ref[begin:end, :],
            (((1,), (1,)), ((), ())),
            preferred_element_type=jnp.float32,
        )
        whole = -(-size // LANES) * LANES
        picked[:, begin : begin + size] = both
        return whole // LANES

    def summed(tile, last):
        at = tile * LANES
        near = jnp.take_along_axis(picked[rows:, at : at + LANES], shifted & (LANES - 1), axis=1)
        return near

    loads[1].wait()
    first_tiles = level_one(0, rows)
    near = [summed(tile, False) for tile in range(halo_tiles)]
    level_tiles = []
    for tile in range(halo_tiles):
        at = tile * LANES
        if tile + 1 < halo_tiles:
            moved = jnp.where(shifted < LANES, near[tile], near[tile + 1])
            sent = rounded(picked[0:rows, at : at + LANES] + moved)
        else:
            moved = near[tile]
            sent = rounded(picked[0:rows, at : at + LANES] + moved)
            edge = pltpu.roll(picked[rows:, 0:LANES], LANES - 1, axis=1)
            sent = jnp.where(lane_rows == LANES - 1, edge, sent)
        halo_out[:, at : at + LANES] = sent.astype(jnp.bfloat16)

    pl.semaphore_wait(barrier, owners - 1)
    back = pltpu.make_async_remote_copy(
        src_ref=halo_out,
        dst_ref=halo_in,
        send_sem=halo_sem.at[0],
        recv_sem=halo_sem.at[1],
        device_id={"sub": lax.rem(me + owners - 1, owners)},
        device_id_type=MESH,
    )

    @pl.when(me > 0)
    def _():
        back.start()

    level_one(rows, window)
    count = -(-window // LANES)
    near = [summed(tile, False) for tile in range(count)]
    previous = None
    for tile in range(count):
        at = tile * LANES
        if tile + 1 < count:
            moved = jnp.where(shifted < LANES, near[tile], near[tile + 1])
        else:
            inside = shifted < window - at
            moved = jnp.where(inside, near[tile], 0.0)
        done = rounded(picked[0:rows, at : at + LANES] + moved)
        done = pltpu.roll(done, pad, axis=1)
        if tile == 0:
            tables[0, :, 0:LANES] = done
        else:
            tables[0, :, at : at + LANES] = jnp.where(lane_rows < pad, previous, done)
        previous = done

    sublane = lax.broadcasted_iota(jnp.int32, (rows, LANES), 0)
    for level_num in range(2, levels + 1):
        span_rows = 2 ** (level_num - 1)
        child_rows = widest_shift(level_num)
        column = 3 * (level_num - 1)
        starts = 2 * child_rows * (sublane >> (level_num - 1))
        lower = jnp.broadcast_to(turned[:, column : column + 1], (rows, LANES)).astype(jnp.int32)
        upper = jnp.broadcast_to(turned[:, column + 1 : column + 2], (rows, LANES))
        amount = jnp.broadcast_to(turned[:, column + 2 : column + 3], (rows, LANES))
        lower_at[level_num - 2] = (starts + lower) & (GROUP - 1)
        upper_at[level_num - 2] = (starts + child_rows + upper.astype(jnp.int32)) & (GROUP - 1)
        lane_at[level_num - 1] = lane_rows + amount.astype(jnp.int32)

    def merge(level_num, begin, end, given, keep):
        span_rows = 2 ** (level_num - 1)
        pairs = 2 * GROUP

        def one(row, low, high):
            at_low = lower_at[level_num - 2, pl.ds(row, GROUP), :]
            at_high = upper_at[level_num - 2, pl.ds(row, GROUP), :]
            reach = lane_at[level_num - 1, pl.ds(row, GROUP), :]
            inside = reach < LANES
            within = reach & (LANES - 1)
            sources = min(end + 1, given) - begin
            moved = []
            for tile in range(begin, begin + sources):
                at = tile * LANES
                value = tables[level_num - 2, pl.ds(high, GROUP), at : at + LANES]
                value = jnp.take_along_axis(value, at_high, axis=0)
                moved.append(jnp.take_along_axis(value, within, axis=1))
            results = []
            for tile in range(begin, end):
                at = tile * LANES
                value = tables[level_num - 2, pl.ds(low, GROUP), at : at + LANES]
                value = jnp.take_along_axis(value, at_low, axis=0)
                here = moved[tile - begin]
                after = moved[min(tile - begin + 1, sources - 1)]
                results.append(value + jnp.where(inside, here, after))
            return results

        def step(index, carry):
            row = pl.multiple_of(index * pairs, pairs)
            if span_rows < pairs:
                places = [(row, row), (row + GROUP, row + GROUP)]
            else:
                wide = span_rows // pairs
                low = (index // wide) * span_rows + (index % wide) * GROUP
                high = low + span_rows // 2
                low = pl.multiple_of(low, GROUP)
                high = pl.multiple_of(high, GROUP)
                places = [(low, high), (low, high)]
            results = [
                one(pl.multiple_of(row + part * GROUP, GROUP), low, high)
                for part, (low, high) in enumerate(places)
            ]
            for tile in range(begin, end):
                keep(row, tile, results[0][tile - begin], results[1][tile - begin])
            return carry

        lax.fori_loop(0, rows // pairs, step, 0, unroll=2)

    def to_table(level_num):
        def keep(row, tile, upper_half, lower_half):
            at = tile * LANES
            tables[level_num - 1, pl.ds(row, GROUP), at : at + LANES] = rounded(upper_half)
            tables[level_num - 1, pl.ds(row + GROUP, GROUP), at : at + LANES] = rounded(lower_half)

        return keep

    def to_output(target, first_tile):
        def keep(row, tile, upper_half, lower_half):
            at = (tile - first_tile) * LANES
            block = jnp.concatenate([upper_half, lower_half], axis=0)
            target[pl.ds(row, 2 * GROUP), at : at + LANES] = block.astype(jnp.bfloat16)

        return keep

    edge = early_tiles * LANES
    given = own_tiles
    for level_num in range(2, levels + 1):
        need = -(-(edge + still_to_come(level_num, levels)) // LANES)
        last = level_num == levels
        merge(
            level_num, 0, need, given, to_output(early_out, 0) if last else to_table(level_num)
        )
        given = need

    def spread(source, target, send_sem, recv_sem, some):
        copies = []
        for apart in range(1, owners):
            to = lax.rem(me + apart, owners)
            base = pl.multiple_of(reversed_index(to, bits) * held, held)
            copy = pltpu.make_async_remote_copy(
                src_ref=source.at[pl.ds(base, held)],
                dst_ref=target.at[me],
                send_sem=send_sem.at[apart],
                recv_sem=recv_sem.at[apart],
                device_id={"sub": to},
                device_id_type=MESH,
            )
            copies.append((copy, apart))

            if some:

                @pl.when(me < owners - 1)
                def _():
                    copy.start()

            else:
                copy.start()
        base = pl.multiple_of(reversed_index(me, bits) * held, held)
        target[me] = source[pl.ds(base, held), :]
        return copies

    early = spread(early_out, early_in, early_send, early_recv, False)

    @pl.when(me < owners - 1)
    def _():
        back.wait_recv()

    @pl.when(me > 0)
    def _():
        back.wait_send()

    for tile in range(halo_tiles):
        at = (own_tiles + tile) * LANES
        tables[0, :, at : at + LANES] = halo_in[:, tile * LANES : (tile + 1) * LANES].astype(
            jnp.float32
        )
    at = (own_tiles - 1) * LANES
    extra = jnp.where(
        lane_at[0] >= LANES, halo_in[:, (halo_tiles - 1) * LANES :].astype(jnp.float32), 0.0
    )
    tables[0, :, at : at + LANES] = rounded(tables[0, :, at : at + LANES] + extra)
    given = all_tiles
    for level_num in range(2, levels + 1):
        coming = still_to_come(level_num, levels)
        begin = (edge + coming) // LANES
        end = -(-(own_tiles * LANES + coming) // LANES)
        last = level_num == levels
        merge(
            level_num,
            begin,
            end,
            given,
            to_output(late_out, early_tiles) if last else to_table(level_num),
        )
        given = end
    late = spread(late_out, late_in, late_send, late_recv, True)

    for load in loads[3:]:
        load.wait()
    for copy, apart in early:
        copy.wait()
    for copy, apart in late:

        @pl.when(me < owners - 1)
        def _():
            copy.wait_send()

        @pl.when(lax.rem(me + owners - apart, owners) < owners - 1)
        def _():
            copy.wait_recv()

    wide_lane = lax.broadcasted_iota(jnp.int32, (held, LANES), 1)
    pieces = [[] for _ in range(fold_size)]
    for source in range(owners):
        offset = window * source - pad
        whole, part = offset // LANES, offset % LANES
        for tile in range(own_tiles):
            spots = []
            from_lane = pad if tile == 0 else 0
            spots.append((whole + tile, max(part, from_lane + part), LANES))
            spots.append((whole + tile + 1, max(0, from_lane + part - LANES), part))
            for fold, begin, end in spots:
                if 0 <= fold < fold_size and begin < end:
                    pieces[fold].append((begin, source, tile, part))
    rolled = {}

    def rolled_tile(source, tile, part):
        if (source, tile) not in rolled:
            if tile < early_tiles:
                value = early_in[source, :, tile * LANES : (tile + 1) * LANES]
            else:
                at = (tile - early_tiles) * LANES
                value = late_in[source, :, at : at + LANES]
            value = value.astype(jnp.float32)
            if part:
                value = pltpu.roll(value, part, axis=1)
            rolled[source, tile] = value
        return rolled[source, tile]

    for fold in range(fold_size):
        value = None
        for begin, source, tile, part in sorted(pieces[fold]):
            piece = rolled_tile(source, tile, part)
            value = piece if value is None else jnp.where(wide_lane < begin, value, piece)
        folded[fold * held : (fold + 1) * held, :] = value

    cosine, sine = twist_ref[0], twist_ref[1]
    for series in range(0, held, 2):
        pair = jnp.concatenate(
            [folded[pl.ds(series + side, fold_size, stride=held), :] for side in range(2)], axis=1
        )
        spun = jnp.dot(
            first_ref[...], pair.astype(jnp.bfloat16), preferred_element_type=jnp.float32
        )
        for side in range(2):
            real = spun[0:fold_size, side * LANES : (side + 1) * LANES]
            imag = spun[fold_size:, side * LANES : (side + 1) * LANES]
            at = (series + side) * fold_size
            twisted[at : at + fold_size, 0:LANES] = (real * cosine + imag * sine).astype(
                jnp.bfloat16
            )
            twisted[at : at + fold_size, LANES:] = (imag * cosine - real * sine).astype(
                jnp.bfloat16
            )
    half = fold_size
    scale = 1.0 / (length * channels)
    small_lane = lax.broadcasted_iota(jnp.int32, (half // 2, LANES), 1)
    for series in range(0, held, 4):
        at = series * fold_size
        waves = lax.dot_general(
            third_ref[...],
            twisted[at : at + 4 * fold_size, :],
            (((1,), (1,)), ((), ())),
            preferred_element_type=jnp.float32,
        )
        power = (waves[0:half] * waves[0:half] + waves[half:] * waves[half:]) * scale
        for side in range(2):
            even = power[0 : half // 2, side * LANES : (side + 1) * LANES]
            odd = power[half // 2 :, side * LANES : (side + 1) * LANES]
            left = jnp.where(small_lane < fold_size, even, pltpu.roll(odd, fold_size, axis=1))
            right = jnp.where(small_lane < fold_size, pltpu.roll(even, fold_size, axis=1), odd)
            spot = (series + 2 * side) * (half // 2)
            powers[spot : spot + half // 2, :] = left
            powers[spot + half // 2 : spot + half, :] = right
    for block in range(0, held, GROUP):
        for tile in range(half // 2):
            out_ref[block : block + GROUP, tile * LANES : (tile + 1) * LANES] = powers[
                pl.ds(block * (half // 2) + tile, GROUP, stride=half // 2), :
            ]


def local_sliced(samples, channel_order, merge_table):
    owners = lax.axis_size("sub")
    window, channels = samples.shape
    levels, _, rows = merge_table.shape
    held = rows // owners
    length = owners * (window - held)
    fold_size = length // LANES
    pad = -window % LANES
    own_tiles = (window + pad) // LANES
    halo_tiles = rows // LANES
    early_tiles = own_tiles - halo_tiles
    order = channel_order.reshape(1, channels)
    first_table, twist, third_table = transform_tables(fold_size, length)
    return pl.pallas_call(
        functools.partial(merge_kernel, owners, length),
        out_shape=jax.ShapeDtypeStruct((held, 64 * fold_size), jnp.float32),
        in_specs=[pl.BlockSpec(memory_space=pl.ANY)] * 6,
        out_specs=pl.BlockSpec(memory_space=pltpu.VMEM),
        scratch_shapes=[
            pltpu.VMEM((1, channels), jnp.int32),
            pltpu.VMEM((levels, 3, rows), jnp.int32),
            pltpu.VMEM((window, channels), jnp.bfloat16),
            pltpu.VMEM(first_table.shape, jnp.bfloat16),
            pltpu.VMEM(twist.shape, jnp.float32),
            pltpu.VMEM(third_table.shape, jnp.bfloat16),
            pltpu.VMEM((channels, LANES), jnp.float32),
            pltpu.VMEM((-(-3 * levels // 8) * 8, rows), jnp.float32),
            pltpu.VMEM((channels, channels), jnp.bfloat16),
            pltpu.VMEM((levels - 1, rows, LANES), jnp.int32),
            pltpu.VMEM((levels - 1, rows, LANES), jnp.int32),
            pltpu.VMEM((levels, rows, LANES), jnp.int32),
            pltpu.VMEM((channels, own_tiles * LANES), jnp.float32),
            pltpu.VMEM((levels - 1, rows, (own_tiles + halo_tiles) * LANES), jnp.float32),
            pltpu.VMEM((rows, rows), jnp.bfloat16),
            pltpu.VMEM((rows, rows), jnp.bfloat16),
            pltpu.VMEM((rows, early_tiles * LANES), jnp.bfloat16),
            pltpu.VMEM((rows, rows), jnp.bfloat16),
            pltpu.VMEM((owners, held, early_tiles * LANES), jnp.bfloat16),
            pltpu.VMEM((owners, held, rows), jnp.bfloat16),
            pltpu.VMEM((held * fold_size, LANES), jnp.float32),
            pltpu.VMEM((held * fold_size, 2 * LANES), jnp.bfloat16),
            pltpu.VMEM((held * fold_size // 2, LANES), jnp.float32),
            pltpu.SemaphoreType.DMA((2,)),
            pltpu.SemaphoreType.DMA((owners,)),
            pltpu.SemaphoreType.DMA((owners,)),
            pltpu.SemaphoreType.DMA((owners,)),
            pltpu.SemaphoreType.DMA((owners,)),
            pltpu.SemaphoreType.DMA((6,)),
        ],
        compiler_params=pltpu.CompilerParams(
            vmem_limit_bytes=48 * 1024 * 1024, collective_id=0, has_side_effects=True
        ),
        name="merge_rows",
    )(order, merge_table, samples, first_table, twist, third_table)


def is_sliced(window, channels, owners, rows, levels):
    held = rows // owners
    length = owners * (window - held)
    return (
        held == 16
        and window % 16 == 0
        and rows % LANES == 0
        and channels == 2 * rows
        and rows == 2 ** (levels - 1)
        and length == 64 * LANES
        and window > 2 * rows
    )


def local_any(samples, channel_order, merge_table):
    window, channels = samples.shape
    levels, _, rows = merge_table.shape
    if is_sliced(window, channels, lax.axis_size("sub"), rows, levels):
        return local_sliced(samples, channel_order, merge_table)
    return local(samples, channel_order, merge_table)


def solution(mesh):
    in_specs = (P(("groups", "sub"), None), P(), P())
    out_specs = P(("groups", "sub"), None)
    return jax.shard_map(local_any, mesh=mesh, in_specs=in_specs, out_specs=out_specs, check_vma=False)
```

time: 26.8 us -> 40.1 us (1.50)
  Pallas kernels: 21.9 us -> 34.1 us
  local copies, waits for them, and re-layouts: 2.16 us -> 5.64 us
  matrix products: 2.38 us -> 0 us
    pallas_call x1, Pallas kernels: 21.9 us -> 34.1 us  [local_sliced(): pl.pallas_call(functools.partial(merge_kernel, owners, length), out_shape...]
    unnamed x0 -> x13, local copies, waits for them, and re-layouts: none -> 5.64 us
    dot_general x6 -> x0, matrix products: 2.38 us -> none  [the longest x1 0.43 us: spectrum(): jnp.einsum('rkn,nj->rjk', twisted_re, sin_three, preferred_element_type=j...]
    transpose x1 -> x0, local copies, waits for them, and re-layouts: 1.1 us -> none  [local_sliced(): series = blocks.transpose(1, 0, 2).reshape(held, owners * length)]
    reshape x1 -> x0, local copies, waits for them, and re-layouts: 0.89 us -> none  [spectrum(): return power.reshape(row_count, 64 * fold_size)]
where the time goes in v1:
time: 40.1 us; the launch traced here: 39.7 us
  Pallas kernels  34.1 us (85%)
  local copies, waits for them, and re-layouts  5.64 us (14%)
    pallas_call x1, Pallas kernels, local_sliced(): pl.pallas_call(functools.partial(merge_kernel, owners, length), out_shape...  34.1 us
    unnamed x13, local copies, waits for them, and re-layouts  5.64 us

profile of v1, /device:TPU:0, one launch (start us, length us, event | category | flops | bytes accessed | tf_op | source)
XLA Modules:
  0.0 39.7 jit_solution(16014796607789427271)
XLA Ops:
  0.0 0.0 copy-start
  0.0 1.0 %copy-done = bf16[528,512]{1,0:T(8,128)(2,1)S(1)} copy-done((bf16[528,512]{1,0:T(8,128)(2,1)S(1)}, bf16[528,512]{1,0:T(8,128)(2,1)}, u32[]{:S(2)}) %copy-start) | copy-done | bytes 540696
  1.0 0.0 copy-start.1
  1.1 0.8 %copy-done.1 = bf16[128,256]{1,0:T(8,128)(2,1)S(1)} copy-done((bf16[128,256]{1,0:T(8,128)(2,1)S(1)}, bf16[128,256]{1,0:T(8,128)(2,1)}, u32[]{:S(2)}) %copy-start.1) | copy-done | bytes 65560
  1.9 0.0 copy-start.2
  1.9 0.8 %copy-done.2 = f32[2,64,128]{2,1,0:T(8,128)S(1)} copy-done((f32[2,64,128]{2,1,0:T(8,128)S(1)}, f32[2,64,128]{2,1,0:T(8,128)}, u32[]{:S(2)}) %copy-start.2) | copy-done | bytes 65560
  2.7 0.0 copy-start.3
  2.7 0.8 %copy-done.3 = s32[9,3,256]{2,1,0:T(4,128)S(1)} copy-done((s32[9,3,256]{2,1,0:T(4,128)S(1)}, s32[9,3,256]{2,1,0:T(4,128)}, u32[]{:S(2)}) %copy-start.3) | copy-done | bytes 27672
  3.5 0.0 copy-start.4
  3.5 0.8 %copy-done.4 = bf16[128,64]{1,0:T(8,128)(2,1)S(1)} copy-done((bf16[128,64]{1,0:T(8,128)(2,1)S(1)}, bf16[128,64]{1,0:T(8,128)(2,1)}, u32[]{:S(2)}) %copy-start.4) | copy-done | bytes 16408
  4.3 0.0 copy-start.5
  4.3 0.7 %copy-done.5 = s32[512]{0:T(512)S(1)} copy-done((s32[512]{0:T(512)S(1)}, s32[512]{0:T(512)}, u32[]{:S(2)}) %copy-start.5) | copy-done | bytes 2072
  4.9 34.1 %merge_rows.1 = f32[16,4096]{1,0:T(8,128)S(1)} custom-call(s32[1,512]{1,0:T(1,128)S(1)} %bitcast.1, s32[9,3,256]{2,1,0:T(4,128)S(1)} %copy-done.3, bf16[528,512]{1,0:T(8,128)(2,1)S(1)} %copy-done, bf16[128,64]{1,0:T(8,128)(2,1)S(1)} %copy-done.4, f32[2,64,128]{2,1,0:T(8,128)S(1)} %copy-done.2, bf16[128,256]{1,0:T(8,128)(2,1)S(1)} %copy-done.1), custom_call_target="tpu_custom_call" | custom-call | tf_op jit(solution)/shard_map/merge_rows/pallas_call | solution.py:611
  39.0 0.7 %copy.8 = f32[16,4096]{1,0:T(8,128)} copy(f32[16,4096]{1,0:T(8,128)S(1)} %merge_rows.1) | data formatting | bytes 524288
Async XLA Ops:
  0.0 1.0 %copy-start = (bf16[528,512]{1,0:T(8,128)(2,1)S(1)}, bf16[528,512]{1,0:T(8,128)(2,1)}, u32[]{:S(2)}) copy-start(bf16[528,512]{1,0:T(8,128)(2,1)} %own_hbm.1) | copy-start | bytes 1622020
  1.0 0.8 %copy-start.1 = (bf16[128,256]{1,0:T(8,128)(2,1)S(1)}, bf16[128,256]{1,0:T(8,128)(2,1)}, u32[]{:S(2)}) copy-start(bf16[128,256]{1,0:T(8,128)(2,1)} %constant.8.clone.third_hbm) | copy-start | bytes 196612
  1.9 0.8 %copy-start.2 = (f32[2,64,128]{2,1,0:T(8,128)S(1)}, f32[2,64,128]{2,1,0:T(8,128)}, u32[]{:S(2)}) copy-start(f32[2,64,128]{2,1,0:T(8,128)} %constant.7.clone.twist_hbm) | copy-start | bytes 196612
  2.7 0.8 %copy-start.3 = (s32[9,3,256]{2,1,0:T(4,128)S(1)}, s32[9,3,256]{2,1,0:T(4,128)}, u32[]{:S(2)}) copy-start(s32[9,3,256]{2,1,0:T(4,128)} %table_hbm.1) | copy-start | bytes 82948
  3.5 0.8 %copy-start.4 = (bf16[128,64]{1,0:T(8,128)(2,1)S(1)}, bf16[128,64]{1,0:T(8,128)(2,1)}, u32[]{:S(2)}) copy-start(bf16[128,64]{1,0:T(8,128)(2,1)} %constant.6.clone.first_hbm) | copy-start | bytes 49156
  4.3 0.7 %copy-start.5 = (s32[512]{0:T(512)S(1)}, s32[512]{0:T(512)}, u32[]{:S(2)}) copy-start(s32[512]{0:T(512)} %param.7) | copy-start | bytes 6148

commit v2 on v1

v2 whole, which is shorter than its diff:
```python
import functools
import math

import jax
import jax.numpy as jnp
import numpy as np
from jax import lax
from jax.experimental import pallas as pl
from jax.experimental.pallas import tpu as pltpu
from jax.sharding import PartitionSpec as P

LOCAL = 5
MESH = pl.DeviceIdType.MESH
CH_DEV = 32
SAMPLES = 8192


def from_partner(block, axis, apart):
    count = lax.axis_size(axis)
    route = []
    for low in range(count):
        high = low | 1 << apart
        if high != low and high < count:
            route += [(low, high), (high, low)]
    return lax.ppermute(block, axis, route)


def delay_rows(values, shifts, margin, time_axis):
    length = values.shape[time_axis]
    moved = values
    for bit_num in range(max(1, margin.bit_length())):
        offset = 2**bit_num
        rolled = jnp.pad(moved[:, offset:], ((0, 0), (0, offset)))
        flagged = shifts >> bit_num & 1 == 1
        flagged = flagged[:, None]
        moved = jnp.where(flagged, rolled, moved)
    return moved


def merge_level(current, entries, child_rows, span_rows, time_axis):
    outputs = jnp.arange(entries.shape[1], dtype=jnp.int32)
    starts = 2 * child_rows * (outputs // span_rows)
    lower_rows = jnp.take(current, starts + entries[0], axis=1 - time_axis)
    upper_rows = jnp.take(current, starts + child_rows + entries[1], axis=1 - time_axis)
    moved_rows = delay_rows(upper_rows, entries[2], child_rows, time_axis)
    return (lower_rows.astype(jnp.float32) + moved_rows.astype(jnp.float32)).astype(jnp.bfloat16)


def spectrum(delays, channels):
    row_count = delays.shape[0]
    length = delays.shape[1]
    fold_size = length // 128
    first_index = jnp.arange(fold_size, dtype=jnp.int32)
    lane_index = jnp.arange(128, dtype=jnp.int32)
    half_index = jnp.arange(64, dtype=jnp.int32)
    angle_one = (
        2.0
        * math.pi
        / fold_size
        * (first_index[:, None] * first_index[None, :] % fold_size).astype(jnp.float32)
    )
    cos_one = jnp.cos(angle_one).astype(jnp.bfloat16)
    sin_one = jnp.sin(angle_one).astype(jnp.bfloat16)
    angle_two = (
        2.0
        * math.pi
        / length
        * (first_index[:, None] * lane_index[None, :] % length).astype(jnp.float32)
    )
    twist_cos = jnp.cos(angle_two)
    twist_sin = jnp.sin(angle_two)
    angle_three = (
        2.0 * math.pi / 128 * (lane_index[:, None] * half_index[None, :] % 128).astype(jnp.float32)
    )
    cos_three = jnp.cos(angle_three).astype(jnp.bfloat16)
    sin_three = jnp.sin(angle_three).astype(jnp.bfloat16)
    series = delays.reshape(row_count, fold_size, 128)
    first_re = jnp.einsum("kn,rnm->rkm", cos_one, series, preferred_element_type=jnp.float32)
    first_im = -jnp.einsum("kn,rnm->rkm", sin_one, series, preferred_element_type=jnp.float32)
    twisted_re = (first_re * twist_cos + first_im * twist_sin).astype(jnp.bfloat16)
    twisted_im = (first_im * twist_cos - first_re * twist_sin).astype(jnp.bfloat16)
    out_re = jnp.einsum(
        "rkn,nj->rjk", twisted_re, cos_three, preferred_element_type=jnp.float32
    ) + jnp.einsum("rkn,nj->rjk", twisted_im, sin_three, preferred_element_type=jnp.float32)
    out_im = jnp.einsum(
        "rkn,nj->rjk", twisted_im, cos_three, preferred_element_type=jnp.float32
    ) - jnp.einsum("rkn,nj->rjk", twisted_re, sin_three, preferred_element_type=jnp.float32)
    power = (out_re * out_re + out_im * out_im) / (length * channels)
    return power.reshape(row_count, 64 * fold_size)


def local(samples, channel_order, merge_table):
    owners = lax.axis_size("sub")
    owner_index = lax.axis_index("sub")
    owned_rows = CH_DEV // 2
    quarter = CH_DEV // 4
    window = samples.shape[0]
    channels = samples.shape[1]
    ordered = jnp.take(samples, channel_order, axis=1).T.reshape(owners, CH_DEV, window)
    current = lax.all_to_all(ordered, "sub", split_axis=0, concat_axis=2, tiled=True).reshape(
        CH_DEV, window * owners
    )
    for level_num in range(1, LOCAL + 1):
        entries = lax.dynamic_slice_in_dim(
            merge_table[level_num - 1], owner_index * owned_rows, owned_rows, 1
        )
        current = merge_level(
            current, entries, max(1, 2 ** (level_num - 2)), 2 ** (level_num - 1), 1
        )
    block_index = jnp.zeros((), jnp.int32)
    for bit_num in range(owners.bit_length() - 1):
        level_num = LOCAL + bit_num + 1
        half_bit = owner_index >> bit_num & 1
        block_index = block_index * 2 + half_bit
        span_rows = owned_rows * 2 ** (bit_num + 1)
        child_rows = span_rows // 2
        subband = owner_index >> bit_num + 1
        entries = lax.dynamic_slice_in_dim(
            merge_table[level_num - 1],
            subband * span_rows + owned_rows * block_index,
            owned_rows,
            1,
        )
        kept_rows = lax.dynamic_slice_in_dim(current, half_bit * quarter, quarter, 0)
        sent_rows = lax.dynamic_slice_in_dim(current, (1 - half_bit) * quarter, quarter, 0)
        partner = from_partner(sent_rows, "sub", bit_num)
        row_base = quarter * block_index
        is_low = half_bit == 0
        lower_part = jnp.where(is_low, kept_rows, partner)
        upper_part = jnp.where(is_low, partner, kept_rows)
        lower_rows = jnp.take(lower_part, entries[0] - row_base, axis=0)
        upper_rows = jnp.take(upper_part, entries[1] - row_base, axis=0)
        moved_rows = delay_rows(upper_rows, entries[2], child_rows, 1)
        current = (lower_rows.astype(jnp.float32) + moved_rows.astype(jnp.float32)).astype(
            jnp.bfloat16
        )
    return spectrum(current[:, :SAMPLES], channels)


LANES = 128
GROUP = 8


def widest_shift(level_num):
    return max(1, 2 ** (level_num - 2))


def still_to_come(level_num, levels):
    return sum(widest_shift(later) for later in range(level_num + 1, levels + 1))


def gathered(values, places, axis):
    other = 1 - axis
    numbers = lax.GatherDimensionNumbers(
        offset_dims=(),
        collapsed_slice_dims=(axis,),
        start_index_map=(axis,),
        operand_batching_dims=(other,),
        start_indices_batching_dims=(other,),
    )
    return lax.gather(
        values,
        places[..., None],
        numbers,
        slice_sizes=(1, 1),
        mode=lax.GatherScatterMode.PROMISE_IN_BOUNDS,
    )


def transform_tables(fold_size, length):
    first_index = np.arange(fold_size)
    lane_index = np.arange(LANES)
    half_index = np.concatenate([np.arange(0, 64, 2), np.arange(1, 64, 2)])
    unit = np.float32(2.0 * math.pi)

    def angles(left, right, period):
        turns = (left[:, None] * right[None, :]) % period
        return (unit / np.float32(period)) * turns.astype(np.float32)

    one = angles(first_index, first_index, fold_size)
    first_table = np.concatenate([np.cos(one), -np.sin(one)], axis=0)
    two = angles(first_index, lane_index, length)
    twist = np.stack([np.cos(two), np.sin(two)])
    three = angles(half_index, lane_index, LANES)
    cos_three, sin_three = np.cos(three), np.sin(three)
    third_table = np.concatenate(
        [
            np.concatenate([cos_three, sin_three], axis=1),
            np.concatenate([-sin_three, cos_three], axis=1),
        ],
        axis=0,
    )
    return (
        jnp.asarray(first_table, jnp.bfloat16),
        jnp.asarray(twist, jnp.float32),
        jnp.asarray(third_table, jnp.bfloat16),
    )


def one_hot(row_index, depth):
    rows = lax.broadcasted_iota(jnp.int32, (depth, row_index.shape[1]), 0)
    return (rows == row_index).astype(jnp.float32).astype(jnp.bfloat16)


def floor_16(count):
    return count // 16 * 16


def ceil_16(count):
    return -(-count // 16) * 16


def merge_kernel(
    owners,
    length,
    order_hbm,
    table_hbm,
    own_hbm,
    first_hbm,
    twist_hbm,
    third_hbm,
    out_ref,
    order_ref,
    table_ref,
    own_ref,
    first_ref,
    twist_ref,
    third_ref,
    split,
    choose,
    choices,
    picked,
    tables,
    halo_out,
    placed,
    early_out,
    late_out,
    early_in,
    late_in,
    folded,
    twisted,
    powers,
    halo_sem,
    early_send,
    early_recv,
    late_send,
    late_recv,
    load_sem,
):
    levels, _, rows = table_ref.shape
    window, channels = own_ref.shape
    held = rows // owners
    fold_size = length // LANES
    me = lax.axis_index("sub")
    bits = owners.bit_length() - 1

    loads = [
        pltpu.make_async_copy(source, target, load_sem.at[place])
        for place, (source, target) in enumerate(
            [
                (order_hbm, order_ref),
                (table_hbm, table_ref),
                (own_hbm, own_ref),
                (first_hbm, first_ref),
                (twist_hbm, twist_ref),
                (third_hbm, third_ref),
            ]
        )
    ]
    for load in loads:
        load.start()
    barrier = pltpu.get_barrier_semaphore()
    for apart in range(1, owners):
        pl.semaphore_signal(
            barrier, inc=1, device_id={"sub": lax.rem(me + apart, owners)}, device_id_type=MESH
        )

    column = lax.broadcasted_iota(jnp.int32, (1, channels), 1)
    split[...] = one_hot(
        jnp.where(column < rows, 2 * column, 2 * (column - rows) + 1), channels
    )
    loads[0].wait()
    order = jnp.broadcast_to(order_ref[...], (16, channels))
    side = lax.broadcasted_iota(jnp.int32, (16, channels), 0)
    digits = jnp.where(side == 0, order >> 6, order & 63).astype(jnp.float32)
    digits = jnp.dot(
        digits.astype(jnp.bfloat16), split[...], preferred_element_type=jnp.float32
    ).astype(jnp.int32)
    choose[...] = one_hot(digits[0:1] * 64 + digits[1:2], channels)

    lane = lax.broadcasted_iota(jnp.int32, (1, LANES), 1)
    sublane = lax.broadcasted_iota(jnp.int32, (GROUP, LANES), 0)

    def combine(level_num, begin, end, given):
        span_rows = 2 ** (level_num - 1)
        columns = []
        for base in range(0, rows, LANES):
            place = (lane + base) % span_rows // 16
            static = base % span_rows // 16
            amount = table_ref[level_num - 1][2:3, base : base + LANES]
            reach = sublane + (amount - GROUP * place)
            inside = reach < GROUP
            turn = reach & (GROUP - 1)
            steps = max(0, min(span_rows, LANES).bit_length() - 5)
            top = end + GROUP + GROUP * (static + 2**steps - 1)
            bottom = begin + GROUP * static
            upper = picked[level_num - 1][bottom : min(top, given), rows + base : rows + base + LANES]
            if top > given:
                filler = jnp.zeros((top - given, LANES), jnp.float32)
                upper = jnp.concatenate([upper, filler], axis=0)
            for step in range(steps):
                offset = GROUP * 2**step
                flagged = (place - static) >> step & 1 == 1
                size = upper.shape[0]
                flagged = jnp.broadcast_to(flagged, (size - offset, LANES))
                upper = jnp.where(flagged, upper[offset:], upper[: size - offset])
            count = (end - begin) // GROUP
            spun = [
                gathered(upper[GROUP * part : GROUP * (part + 1)], turn, 0)
                for part in range(count + 1)
            ]
            moved = [jnp.where(inside, spun[part], spun[part + 1]) for part in range(count)]
            lower = picked[level_num - 1][begin:end, base : base + LANES]
            columns.append(lower + jnp.concatenate(moved, axis=0))
        return jnp.concatenate(columns, axis=1)

    loads[1].wait()
    loads[2].wait()
    ahead = ceil_16(rows + GROUP)
    picked[0][0:ahead, :] = jnp.dot(
        own_ref[0:ahead, :], choose[...], preferred_element_type=jnp.float32
    )
    near = combine(1, 0, rows, ahead)
    tables[0][0:rows, :] = near.astype(jnp.bfloat16)
    halo_out[0 : rows - 16, :] = near[0 : rows - 16].astype(jnp.bfloat16)
    edge = jnp.broadcast_to(picked[0][0:1, rows:], (16, rows))
    last_row = lax.broadcasted_iota(jnp.int32, (16, rows), 0) == 15
    halo_out[rows - 16 :, :] = jnp.where(last_row, edge, near[rows - 16 :]).astype(jnp.bfloat16)

    pl.semaphore_wait(barrier, owners - 1)
    back = pltpu.make_async_remote_copy(
        src_ref=halo_out,
        dst_ref=tables[0].at[window : window + rows],
        send_sem=halo_sem.at[0],
        recv_sem=halo_sem.at[1],
        device_id={"sub": lax.rem(me + owners - 1, owners)},
        device_id_type=MESH,
    )

    @pl.when(me > 0)
    def _():
        back.start()

    picked[0][ahead:window, :] = jnp.dot(
        own_ref[ahead:window, :], choose[...], preferred_element_type=jnp.float32
    )
    tables[0][rows:window, :] = combine(1, rows, window, window).astype(jnp.bfloat16)

    lanes = lax.broadcasted_iota(jnp.int32, (1, rows), 1)

    def prepare(level_num):
        child_rows = widest_shift(level_num)
        entries = table_ref[level_num - 1]
        starts = 2 * child_rows * (lanes >> (level_num - 1))
        choices[level_num - 2, :, 0:rows] = one_hot(starts + entries[0:1], rows)
        choices[level_num - 2, :, rows:] = one_hot(starts + child_rows + entries[1:2], rows)

    def advance(level_num, source_begin, source_end, begin, end):
        picked[level_num - 1][source_begin:source_end, :] = jnp.dot(
            tables[level_num - 2][source_begin:source_end, :],
            choices[level_num - 2],
            preferred_element_type=jnp.float32,
        )
        tables[level_num - 1][begin:end, :] = combine(
            level_num, begin, end, source_end
        ).astype(jnp.bfloat16)

    valid = window - 1
    ready = window
    starts_late = [floor_16(valid)]
    for level_num in range(2, levels + 1):
        prepare(level_num)
        valid -= widest_shift(level_num)
        end = ceil_16(valid)
        advance(level_num, 0, ready, 0, end)
        ready = end
        starts_late.append(floor_16(valid))
    early = ready

    spots = lax.broadcasted_iota(jnp.int32, (rows, rows), 0)
    shift = held.bit_length() - 1
    wanted = jnp.zeros_like(spots)
    for bit_num in range(bits):
        wanted = wanted | ((spots >> (shift + bit_num) & 1) << (bits - 1 - bit_num))
    wanted = (wanted << shift) + (spots & (held - 1))
    placed[...] = (
        (lax.broadcasted_iota(jnp.int32, (rows, rows), 1) == wanted)
        .astype(jnp.float32)
        .astype(jnp.bfloat16)
    )

    def turn_over(begin, end):
        return lax.dot_general(
            placed[...],
            tables[levels - 1][begin:end, :],
            (((1,), (1,)), ((), ())),
            preferred_element_type=jnp.float32,
        ).astype(jnp.bfloat16)

    def spread(source, target, send_sem, recv_sem, some):
        copies = []
        for apart in range(1, owners):
            to = lax.rem(me + apart, owners)
            copy = pltpu.make_async_remote_copy(
                src_ref=source.at[pl.ds(pl.multiple_of(to * held, held), held)],
                dst_ref=target.at[me],
                send_sem=send_sem.at[apart],
                recv_sem=recv_sem.at[apart],
                device_id={"sub": to},
                device_id_type=MESH,
            )
            copies.append((copy, apart))

            if some:

                @pl.when(me < owners - 1)
                def _():
                    copy.start()

            else:
                copy.start()
        target[me] = source[pl.ds(pl.multiple_of(me * held, held), held), :]
        return copies

    early_out[:, 0:early] = turn_over(0, early)
    early_copies = spread(early_out, early_in, early_send, early_recv, False)

    @pl.when(me < owners - 1)
    def _():
        back.wait_recv()

    @pl.when(me > 0)
    def _():
        back.wait_send()

    fill = tables[0][window - 16 : window, :].astype(jnp.float32)
    edge = tables[0][window + rows - 16 : window + rows, :].astype(jnp.float32)[15:16]
    amount = jnp.broadcast_to(table_ref[0][2:3, :], (16, rows))
    fill = fill + jnp.where(last_row & (amount > 0), jnp.broadcast_to(edge, (16, rows)), 0.0)
    tables[0][window - 16 : window, :] = fill.astype(jnp.bfloat16)
    ready = window + rows
    for level_num in range(2, levels + 1):
        end = ceil_16(window + still_to_come(level_num, levels))
        advance(
            level_num, starts_late[level_num - 2], ready, starts_late[level_num - 1], end
        )
        ready = end
    late_out[...] = turn_over(early, window)
    late_copies = spread(late_out, late_in, late_send, late_recv, True)

    for load in loads[3:]:
        load.wait()
    for copy, apart in early_copies:
        copy.wait()
    for copy, apart in late_copies:

        @pl.when(me < owners - 1)
        def _():
            copy.wait_send()

        @pl.when(lax.rem(me + owners - apart, owners) < owners - 1)
        def _():
            copy.wait_recv()

    wide_lane = lax.broadcasted_iota(jnp.int32, (held, LANES), 1)
    pieces = [[] for _ in range(fold_size)]
    for source in range(owners):
        for late, begin, end in ((False, 0, early), (True, early, window)):
            for at in range(begin, end, LANES):
                fold, part = divmod(window * source + at, LANES)
                count = min(LANES, end - at)
                for where, low, high in (
                    (fold, part, min(LANES, part + count)),
                    (fold + 1, 0, part + count - LANES),
                ):
                    if where < fold_size and low < high:
                        pieces[where].append((low, source, late, at - begin, part))
    rolled = {}

    def rolled_tile(source, late, at, part):
        if (source, late, at) not in rolled:
            value = (late_in if late else early_in)[source, :, at : at + LANES]
            value = value.astype(jnp.float32)
            if part:
                value = pltpu.roll(value, part, axis=1)
            rolled[source, late, at] = value
        return rolled[source, late, at]

    for fold in range(fold_size):
        value = None
        for low, source, late, at, part in sorted(pieces[fold]):
            piece = rolled_tile(source, late, at, part)
            value = piece if value is None else jnp.where(wide_lane < low, value, piece)
        folded[fold * held : (fold + 1) * held, :] = value

    cosine, sine = twist_ref[0], twist_ref[1]
    for series in range(0, held, 2):
        pair = jnp.concatenate(
            [folded[pl.ds(series + side, fold_size, stride=held), :] for side in range(2)], axis=1
        )
        spun = jnp.dot(
            first_ref[...], pair.astype(jnp.bfloat16), preferred_element_type=jnp.float32
        )
        for side in range(2):
            real = spun[0:fold_size, side * LANES : (side + 1) * LANES]
            imag = spun[fold_size:, side * LANES : (side + 1) * LANES]
            at = (series + side) * fold_size
            twisted[at : at + fold_size, 0:LANES] = (real * cosine + imag * sine).astype(
                jnp.bfloat16
            )
            twisted[at : at + fold_size, LANES:] = (imag * cosine - real * sine).astype(
                jnp.bfloat16
            )
    half = fold_size
    scale = 1.0 / (length * channels)
    small_lane = lax.broadcasted_iota(jnp.int32, (half // 2, LANES), 1)
    for series in range(0, held, 4):
        at = series * fold_size
        waves = lax.dot_general(
            third_ref[...],
            twisted[at : at + 4 * fold_size, :],
            (((1,), (1,)), ((), ())),
            preferred_element_type=jnp.float32,
        )
        power = (waves[0:half] * waves[0:half] + waves[half:] * waves[half:]) * scale
        for side in range(2):
            even = power[0 : half // 2, side * LANES : (side + 1) * LANES]
            odd = power[half // 2 :, side * LANES : (side + 1) * LANES]
            left = jnp.where(small_lane < fold_size, even, pltpu.roll(odd, fold_size, axis=1))
            right = jnp.where(small_lane < fold_size, pltpu.roll(even, fold_size, axis=1), odd)
            spot = (series + 2 * side) * (half // 2)
            powers[spot : spot + half // 2, :] = left
            powers[spot + half // 2 : spot + half, :] = right
    for block in range(0, held, GROUP):
        for tile in range(half // 2):
            out_ref[block : block + GROUP, tile * LANES : (tile + 1) * LANES] = powers[
                pl.ds(block * (half // 2) + tile, GROUP, stride=half // 2), :
            ]


def local_sliced(samples, channel_order, merge_table):
    owners = lax.axis_size("sub")
    window, channels = samples.shape
    levels, _, rows = merge_table.shape
    held = rows // owners
    length = owners * (window - held)
    fold_size = length // LANES
    early = window - rows
    whole = window + rows
    order = channel_order.reshape(1, channels)
    first_table, twist, third_table = transform_tables(fold_size, length)
    return pl.pallas_call(
        functools.partial(merge_kernel, owners, length),
        out_shape=jax.ShapeDtypeStruct((held, 64 * fold_size), jnp.float32),
        in_specs=[pl.BlockSpec(memory_space=pl.ANY)] * 6,
        out_specs=pl.BlockSpec(memory_space=pltpu.VMEM),
        scratch_shapes=[
            pltpu.VMEM((1, channels), jnp.int32),
            pltpu.VMEM((levels, 3, rows), jnp.int32),
            pltpu.VMEM((window, channels), jnp.bfloat16),
            pltpu.VMEM(first_table.shape, jnp.bfloat16),
            pltpu.VMEM(twist.shape, jnp.float32),
            pltpu.VMEM(third_table.shape, jnp.bfloat16),
            pltpu.VMEM((channels, channels), jnp.bfloat16),
            pltpu.VMEM((channels, channels), jnp.bfloat16),
            pltpu.VMEM((levels - 1, rows, 2 * rows), jnp.bfloat16),
            [pltpu.VMEM((whole, 2 * rows), jnp.float32)] * levels,
            [pltpu.VMEM((whole, rows), jnp.bfloat16)] * levels,
            pltpu.VMEM((rows, rows), jnp.bfloat16),
            pltpu.VMEM((rows, rows), jnp.bfloat16),
            pltpu.VMEM((rows, -(-early // LANES) * LANES), jnp.bfloat16),
            pltpu.VMEM((rows, rows), jnp.bfloat16),
            pltpu.VMEM((owners, held, -(-early // LANES) * LANES), jnp.bfloat16),
            pltpu.VMEM((owners, held, rows), jnp.bfloat16),
            pltpu.VMEM((held * fold_size, LANES), jnp.float32),
            pltpu.VMEM((held * fold_size, 2 * LANES), jnp.bfloat16),
            pltpu.VMEM((held * fold_size // 2, LANES), jnp.float32),
            pltpu.SemaphoreType.DMA((2,)),
            pltpu.SemaphoreType.DMA((owners,)),
            pltpu.SemaphoreType.DMA((owners,)),
            pltpu.SemaphoreType.DMA((owners,)),
            pltpu.SemaphoreType.DMA((owners,)),
            pltpu.SemaphoreType.DMA((6,)),
        ],
        compiler_params=pltpu.CompilerParams(
            vmem_limit_bytes=62 * 1024 * 1024, collective_id=0, has_side_effects=True
        ),
        name="merge_rows",
    )(order, merge_table, samples, first_table, twist, third_table)


def is_sliced(window, channels, owners, rows, levels):
    held = rows // owners
    length = owners * (window - held)
    return (
        held == 16
        and window % 16 == 0
        and rows % LANES == 0
        and channels == 2 * rows
        and rows == 2 ** (levels - 1)
        and length == 64 * LANES
        and window > 2 * rows
    )


def local_any(samples, channel_order, merge_table):
    window, channels = samples.shape
    levels, _, rows = merge_table.shape
    if is_sliced(window, channels, lax.axis_size("sub"), rows, levels):
        return local_sliced(samples, channel_order, merge_table)
    return local(samples, channel_order, merge_table)


def solution(mesh):
    in_specs = (P(("groups", "sub"), None), P(), P())
    out_specs = P(("groups", "sub"), None)
    return jax.shard_map(local_any, mesh=mesh, in_specs=in_specs, out_specs=out_specs, check_vma=False)
```

time: 40.1 us -> 19.6 us (0.49)
  Pallas kernels: 34.1 us -> 17.7 us
  local copies, waits for them, and re-layouts: 5.64 us -> 1.67 us
    pallas_call x1, Pallas kernels: 34.1 us -> 17.7 us  [local_sliced(): pl.pallas_call(functools.partial(merge_kernel, owners, length), out_shape...]
    unnamed x13 -> x1, local copies, waits for them, and re-layouts: 5.64 us -> 1.67 us
where the time goes in v2:
time: 19.6 us; the launch traced here: 19.4 us
  Pallas kernels  17.7 us (90%)
  local copies, waits for them, and re-layouts  1.67 us (9%)
    pallas_call x1, Pallas kernels, local_sliced(): pl.pallas_call(functools.partial(merge_kernel, owners, length), out_shape...  17.7 us
    unnamed x1, local copies, waits for them, and re-layouts  1.67 us

profile of v2, /device:TPU:0, one launch (start us, length us, event | category | flops | bytes accessed | tf_op | source)
XLA Modules:
  0.0 19.4 jit_solution(2421080891528455338)
XLA Ops:
  0.0 17.7 %merge_rows.1 = f32[16,4096]{1,0:T(8,128)} custom-call(s32[1,512]{1,0:T(1,128)} %bitcast.1, s32[9,3,256]{2,1,0:T(4,128)} %table_hbm.1, bf16[528,512]{1,0:T(8,128)(2,1)} %own_hbm.1, bf16[128,64]{1,0:T(8,128)(2,1)} %constant.6.clone.first_hbm, f32[2,64,128]{2,1,0:T(8,128)} %constant.7.clone.twist_hbm, bf16[128,256]{1,0:T(8,128)(2,1)} %constant.8.clone.third_hbm), custom_call_target="tpu_custom_call" | custom-call | tf_op jit(solution)/shard_map/merge_rows/pallas_call | solution.py:562
  17.7 1.7 %copy.8 = f32[16,4096]{1,0:T(8,128)} copy(f32[16,4096]{1,0:T(8,128)} %merge_rows.1) | data formatting | bytes 524288

commit v3 on v2

--- a/solution.py
+++ b/solution.py
@@ -139,6 +139,8 @@
 
 LANES = 128
 GROUP = 8
+FOLD_PITCH = 24
+POWER_PITCH = 40
 
 
 def widest_shift(level_num):
@@ -270,15 +272,24 @@
     for load in loads:
         load.start()
     barrier = pltpu.get_barrier_semaphore()
-    for apart in range(1, owners):
-        pl.semaphore_signal(
-            barrier, inc=1, device_id={"sub": lax.rem(me + apart, owners)}, device_id_type=MESH
-        )
-
     column = lax.broadcasted_iota(jnp.int32, (1, channels), 1)
-    split[...] = one_hot(
-        jnp.where(column < rows, 2 * column, 2 * (column - rows) + 1), channels
-    )
+    paired = jnp.where(column < rows, 2 * column, 2 * (column - rows) + 1)
+    stripe = channels // owners
+    for apart in range(owners):
+        if apart:
+            pl.semaphore_signal(
+                barrier,
+                inc=1,
+                device_id={"sub": lax.rem(me + apart, owners)},
+                device_id_type=MESH,
+            )
+        split[apart * stripe : (apart + 1) * stripe, :] = one_hot(paired - apart * stripe, stripe)
+    half_rows = rows // 2
+    for level_num in range(1, levels):
+        end = ceil_16(window + still_to_come(level_num, levels))
+        tables[level_num - 1][floor_16(end - half_rows) : end, 0:half_rows] = jnp.zeros(
+            (end - floor_16(end - half_rows), half_rows), jnp.bfloat16
+        )
     loads[0].wait()
     order = jnp.broadcast_to(order_ref[...], (16, channels))
     side = lax.broadcasted_iota(jnp.int32, (16, channels), 0)
@@ -291,10 +302,13 @@
     lane = lax.broadcasted_iota(jnp.int32, (1, LANES), 1)
     sublane = lax.broadcasted_iota(jnp.int32, (GROUP, LANES), 0)
 
-    def combine(level_num, begin, end, given):
+    def combine(level_num, begin, ends, given):
+        ends = ends if isinstance(ends, list) else [ends] * (rows // LANES)
         span_rows = 2 ** (level_num - 1)
         columns = []
         for base in range(0, rows, LANES):
+            end = ends[base // LANES]
+            count = (end - begin) // GROUP
             place = (lane + base) % span_rows // 16
             static = base % span_rows // 16
             amount = table_ref[level_num - 1][2:3, base : base + LANES]
@@ -314,7 +328,6 @@
                 size = upper.shape[0]
                 flagged = jnp.broadcast_to(flagged, (size - offset, LANES))
                 upper = jnp.where(flagged, upper[offset:], upper[: size - offset])
-            count = (end - begin) // GROUP
             spun = [
                 gathered(upper[GROUP * part : GROUP * (part + 1)], turn, 0)
                 for part in range(count + 1)
@@ -322,7 +335,7 @@
             moved = [jnp.where(inside, spun[part], spun[part + 1]) for part in range(count)]
             lower = picked[level_num - 1][begin:end, base : base + LANES]
             columns.append(lower + jnp.concatenate(moved, axis=0))
-        return jnp.concatenate(columns, axis=1)
+        return columns
 
     loads[1].wait()
     loads[2].wait()
@@ -331,30 +344,41 @@
         own_ref[0:ahead, :], choose[...], preferred_element_type=jnp.float32
     )
     near = combine(1, 0, rows, ahead)
-    tables[0][0:rows, :] = near.astype(jnp.bfloat16)
-    halo_out[0 : rows - 16, :] = near[0 : rows - 16].astype(jnp.bfloat16)
-    edge = jnp.broadcast_to(picked[0][0:1, rows:], (16, rows))
-    last_row = lax.broadcasted_iota(jnp.int32, (16, rows), 0) == 15
-    halo_out[rows - 16 :, :] = jnp.where(last_row, edge, near[rows - 16 :]).astype(jnp.bfloat16)
+    last_row = lax.broadcasted_iota(jnp.int32, (16, half_rows), 0) == 15
+    for part, values in enumerate(near):
+        at = part * half_rows
+        tables[0][0:rows, at : at + half_rows] = values.astype(jnp.bfloat16)
+        top = (part + 1) * half_rows
+        halo_out[0 : top - 16, at : at + half_rows] = values[0 : top - 16].astype(jnp.bfloat16)
+        edge = jnp.broadcast_to(picked[0][0:1, rows + at : rows + at + half_rows], (16, half_rows))
+        halo_out[top - 16 : top, at : at + half_rows] = jnp.where(
+            last_row, edge, values[top - 16 : top]
+        ).astype(jnp.bfloat16)
 
     pl.semaphore_wait(barrier, owners - 1)
-    back = pltpu.make_async_remote_copy(
-        src_ref=halo_out,
-        dst_ref=tables[0].at[window : window + rows],
-        send_sem=halo_sem.at[0],
-        recv_sem=halo_sem.at[1],
-        device_id={"sub": lax.rem(me + owners - 1, owners)},
-        device_id_type=MESH,
-    )
+    backs = [
+        pltpu.make_async_remote_copy(
+            src_ref=halo_out.at[0:count, first : first + half_rows],
+            dst_ref=tables[0].at[window : window + count, first : first + half_rows],
+            send_sem=halo_sem.at[part],
+            recv_sem=halo_sem.at[2 + part],
+            device_id={"sub": lax.rem(me + owners - 1, owners)},
+            device_id_type=MESH,
+        )
+        for part, (count, first) in enumerate(((rows, half_rows), (half_rows, 0)))
+    ]
 
     @pl.when(me > 0)
     def _():
-        back.start()
+        for back in backs:
+            back.start()
 
     picked[0][ahead:window, :] = jnp.dot(
         own_ref[ahead:window, :], choose[...], preferred_element_type=jnp.float32
     )
-    tables[0][rows:window, :] = combine(1, rows, window, window).astype(jnp.bfloat16)
+    for part, values in enumerate(combine(1, rows, window, window)):
+        at = part * half_rows
+        tables[0][rows:window, at : at + half_rows] = values.astype(jnp.bfloat16)
 
     lanes = lax.broadcasted_iota(jnp.int32, (1, rows), 1)
 
@@ -365,15 +389,17 @@
         choices[level_num - 2, :, 0:rows] = one_hot(starts + entries[0:1], rows)
         choices[level_num - 2, :, rows:] = one_hot(starts + child_rows + entries[1:2], rows)
 
-    def advance(level_num, source_begin, source_end, begin, end):
+    def advance(level_num, source_begin, source_end, begin, ends):
         picked[level_num - 1][source_begin:source_end, :] = jnp.dot(
             tables[level_num - 2][source_begin:source_end, :],
             choices[level_num - 2],
             preferred_element_type=jnp.float32,
         )
-        tables[level_num - 1][begin:end, :] = combine(
-            level_num, begin, end, source_end
-        ).astype(jnp.bfloat16)
+        for part, values in enumerate(combine(level_num, begin, ends, source_end)):
+            at = part * half_rows
+            tables[level_num - 1][begin : begin + values.shape[0], at : at + half_rows] = (
+                values.astype(jnp.bfloat16)
+            )
 
     valid = window - 1
     ready = window
@@ -437,40 +463,33 @@
 
     @pl.when(me < owners - 1)
     def _():
-        back.wait_recv()
+        for back in backs:
+            back.wait_recv()
 
     @pl.when(me > 0)
     def _():
-        back.wait_send()
-
-    fill = tables[0][window - 16 : window, :].astype(jnp.float32)
-    edge = tables[0][window + rows - 16 : window + rows, :].astype(jnp.float32)[15:16]
-    amount = jnp.broadcast_to(table_ref[0][2:3, :], (16, rows))
-    fill = fill + jnp.where(last_row & (amount > 0), jnp.broadcast_to(edge, (16, rows)), 0.0)
-    tables[0][window - 16 : window, :] = fill.astype(jnp.bfloat16)
+        for back in backs:
+            back.wait_send()
+
+    for part in range(2):
+        at = part * half_rows
+        top = window + (part + 1) * half_rows
+        fill = tables[0][window - 16 : window, at : at + half_rows].astype(jnp.float32)
+        edge = tables[0][top - 16 : top, at : at + half_rows].astype(jnp.float32)[15:16]
+        amount = table_ref[0][2:3, at : at + half_rows]
+        late_edge = last_row & jnp.broadcast_to(amount > 0, (16, half_rows))
+        fill = fill + jnp.where(late_edge, jnp.broadcast_to(edge, (16, half_rows)), 0.0)
+        tables[0][window - 16 : window, at : at + half_rows] = fill.astype(jnp.bfloat16)
     ready = window + rows
     for level_num in range(2, levels + 1):
         end = ceil_16(window + still_to_come(level_num, levels))
+        ends = [end if level_num == levels else ceil_16(end - half_rows), end]
         advance(
-            level_num, starts_late[level_num - 2], ready, starts_late[level_num - 1], end
+            level_num, starts_late[level_num - 2], ready, starts_late[level_num - 1], ends
         )
         ready = end
     late_out[...] = turn_over(early, window)
     late_copies = spread(late_out, late_in, late_send, late_recv, True)
-
-    for load in loads[3:]:
-        load.wait()
-    for copy, apart in early_copies:
-        copy.wait()
-    for copy, apart in late_copies:
-
-        @pl.when(me < owners - 1)
-        def _():
-            copy.wait_send()
-
-        @pl.when(lax.rem(me + owners - apart, owners) < owners - 1)
-        def _():
-            copy.wait_recv()
 
     wide_lane = lax.broadcasted_iota(jnp.int32, (held, LANES), 1)
     pieces = [[] for _ in range(fold_size)]
@@ -484,7 +503,7 @@
                     (fold + 1, 0, part + count - LANES),
                 ):
                     if where < fold_size and low < high:
-                        pieces[where].append((low, source, late, at - begin, part))
+                        pieces[where].append((low, high, source, late, at - begin, part))
     rolled = {}
 
     def rolled_tile(source, late, at, part):
@@ -496,17 +515,48 @@
             rolled[source, late, at] = value
         return rolled[source, late, at]
 
-    for fold in range(fold_size):
-        value = None
-        for low, source, late, at, part in sorted(pieces[fold]):
-            piece = rolled_tile(source, late, at, part)
-            value = piece if value is None else jnp.where(wide_lane < low, value, piece)
-        folded[fold * held : (fold + 1) * held, :] = value
+    def assemble(which):
+        for fold in range(fold_size):
+            some = [piece for piece in sorted(pieces[fold]) if piece[3] == which]
+            if not some:
+                continue
+            where = slice(fold * FOLD_PITCH, fold * FOLD_PITCH + held)
+            value = None
+            if which and len(some) < len(pieces[fold]):
+                value = folded[where, :]
+            for low, high, source, late, at, part in some:
+                piece = rolled_tile(source, late, at, part)
+                if value is None:
+                    value = piece
+                elif high == LANES:
+                    value = jnp.where(wide_lane < low, value, piece)
+                elif low == 0:
+                    value = jnp.where(wide_lane < high, piece, value)
+                else:
+                    value = jnp.where((wide_lane >= low) & (wide_lane < high), piece, value)
+            folded[where, :] = value
+
+    for copy, apart in early_copies:
+        copy.wait()
+    assemble(False)
+    for load in loads[3:]:
+        load.wait()
+    for copy, apart in late_copies:
+
+        @pl.when(me < owners - 1)
+        def _():
+            copy.wait_send()
+
+        @pl.when(lax.rem(me + owners - apart, owners) < owners - 1)
+        def _():
+            copy.wait_recv()
+
+    assemble(True)
 
     cosine, sine = twist_ref[0], twist_ref[1]
     for series in range(0, held, 2):
         pair = jnp.concatenate(
-            [folded[pl.ds(series + side, fold_size, stride=held), :] for side in range(2)], axis=1
+            [folded[pl.ds(series + side, fold_size, stride=FOLD_PITCH), :] for side in range(2)], axis=1
         )
         spun = jnp.dot(
             first_ref[...], pair.astype(jnp.bfloat16), preferred_element_type=jnp.float32
@@ -538,14 +588,18 @@
             odd = power[half // 2 :, side * LANES : (side + 1) * LANES]
             left = jnp.where(small_lane < fold_size, even, pltpu.roll(odd, fold_size, axis=1))
             right = jnp.where(small_lane < fold_size, pltpu.roll(even, fold_size, axis=1), odd)
-            spot = (series + 2 * side) * (half // 2)
+            spot = (series + 2 * side) * POWER_PITCH
             powers[spot : spot + half // 2, :] = left
-            powers[spot + half // 2 : spot + half, :] = right
+            powers[spot + POWER_PITCH : spot + POWER_PITCH + half // 2, :] = right
     for block in range(0, held, GROUP):
         for tile in range(half // 2):
             out_ref[block : block + GROUP, tile * LANES : (tile + 1) * LANES] = powers[
-                pl.ds(block * (half // 2) + tile, GROUP, stride=half // 2), :
+                pl.ds(block * POWER_PITCH + tile, GROUP, stride=POWER_PITCH), :
             ]
+
+
+def in_place(*operands):
+    return [pltpu.with_memory_space_constraint(operand, pltpu.HBM) for operand in operands]
 
 
 def local_sliced(samples, channel_order, merge_table):
@@ -561,7 +615,7 @@
     first_table, twist, third_table = transform_tables(fold_size, length)
     return pl.pallas_call(
         functools.partial(merge_kernel, owners, length),
-        out_shape=jax.ShapeDtypeStruct((held, 64 * fold_size), jnp.float32),
+        out_shape=pltpu.VMEM((held, 64 * fold_size), jnp.float32),
         in_specs=[pl.BlockSpec(memory_space=pl.ANY)] * 6,
         out_specs=pl.BlockSpec(memory_space=pltpu.VMEM),
         scratch_shapes=[
@@ -582,10 +636,10 @@
             pltpu.VMEM((rows, rows), jnp.bfloat16),
             pltpu.VMEM((owners, held, -(-early // LANES) * LANES), jnp.bfloat16),
             pltpu.VMEM((owners, held, rows), jnp.bfloat16),
-            pltpu.VMEM((held * fold_size, LANES), jnp.float32),
+            pltpu.VMEM((FOLD_PITCH * fold_size, LANES), jnp.float32),
             pltpu.VMEM((held * fold_size, 2 * LANES), jnp.bfloat16),
-            pltpu.VMEM((held * fold_size // 2, LANES), jnp.float32),
-            pltpu.SemaphoreType.DMA((2,)),
+            pltpu.VMEM((POWER_PITCH * held, LANES), jnp.float32),
+            pltpu.SemaphoreType.DMA((4,)),
             pltpu.SemaphoreType.DMA((owners,)),
             pltpu.SemaphoreType.DMA((owners,)),
             pltpu.SemaphoreType.DMA((owners,)),
@@ -593,10 +647,10 @@
             pltpu.SemaphoreType.DMA((6,)),
         ],
         compiler_params=pltpu.CompilerParams(
-            vmem_limit_bytes=62 * 1024 * 1024, collective_id=0, has_side_effects=True
+            vmem_limit_bytes=40 * 1024 * 1024, collective_id=0, has_side_effects=True
         ),
         name="merge_rows",
-    )(order, merge_table, samples, first_table, twist, third_table)
+    )(*in_place(order, merge_table, samples, first_table, twist, third_table))
 
 
 def is_sliced(window, channels, owners, rows, levels):
@@ -605,7 +659,7 @@
     return (
         held == 16
         and window % 16 == 0
-        and rows % LANES == 0
+        and rows == 2 * LANES
         and channels == 2 * rows
         and rows == 2 ** (levels - 1)
         and length == 64 * LANES

time: 19.6 us -> 17.8 us (0.908)
  local copies, waits for them, and re-layouts: 1.67 us -> 0.71 us
  Pallas kernels: 17.7 us -> 16.9 us
    unnamed x1, local copies, waits for them, and re-layouts: 1.67 us -> 0.71 us
    pallas_call x1, Pallas kernels: 17.7 us -> 16.9 us  [local_sliced(): pl.pallas_call(functools.partial(merge_kernel, owners, length), out_shape...]
where the time goes in v3:
time: 17.8 us; the launch traced here: 17.6 us
  Pallas kernels  16.9 us (95%)
  local copies, waits for them, and re-layouts  0.71 us (4%)
    pallas_call x1, Pallas kernels, local_sliced(): pl.pallas_call(functools.partial(merge_kernel, owners, length), out_shape...  16.9 us
    unnamed x1, local copies, waits for them, and re-layouts  0.71 us

profile of v3, /device:TPU:0, one launch (start us, length us, event | category | flops | bytes accessed | tf_op | source)
XLA Modules:
  0.0 17.6 jit_solution(10931326153758684949)
XLA Ops:
  0.0 16.9 %merge_rows.1 = f32[16,4096]{1,0:T(8,128)S(1)} custom-call(s32[1,512]{1,0:T(1,128)} %bitcast.1, s32[9,3,256]{2,1,0:T(4,128)} %table_hbm.1, bf16[528,512]{1,0:T(8,128)(2,1)} %own_hbm.1, bf16[128,64]{1,0:T(8,128)(2,1)} %constant.6.clone.first_hbm, f32[2,64,128]{2,1,0:T(8,128)} %constant.7.clone.twist_hbm, bf16[128,256]{1,0:T(8,128)(2,1)} %constant.8.clone.third_hbm), custom_call_target="tpu_custom_call" | custom-call | tf_op jit(solution)/shard_map/merge_rows/pallas_call | solution.py:616
  16.9 0.7 %copy.8 = f32[16,4096]{1,0:T(8,128)} copy(f32[16,4096]{1,0:T(8,128)S(1)} %merge_rows.1) | data formatting | bytes 524288

commit v4 on v3

--- a/solution.py
+++ b/solution.py
@@ -231,6 +231,7 @@
     split,
     choose,
     choices,
+    first_picked,
     picked,
     tables,
     halo_out,
@@ -285,11 +286,11 @@
             )
         split[apart * stripe : (apart + 1) * stripe, :] = one_hot(paired - apart * stripe, stripe)
     half_rows = rows // 2
-    for level_num in range(1, levels):
-        end = ceil_16(window + still_to_come(level_num, levels))
-        tables[level_num - 1][floor_16(end - half_rows) : end, 0:half_rows] = jnp.zeros(
-            (end - floor_16(end - half_rows), half_rows), jnp.bfloat16
-        )
+
+    @pl.when(me == owners - 1)
+    def _():
+        tables[0][window:, :] = jnp.zeros((rows, rows), jnp.bfloat16)
+
     loads[0].wait()
     order = jnp.broadcast_to(order_ref[...], (16, channels))
     side = lax.broadcasted_iota(jnp.int32, (16, channels), 0)
@@ -302,55 +303,61 @@
     lane = lax.broadcasted_iota(jnp.int32, (1, LANES), 1)
     sublane = lax.broadcasted_iota(jnp.int32, (GROUP, LANES), 0)
 
-    def combine(level_num, begin, ends, given):
-        ends = ends if isinstance(ends, list) else [ends] * (rows // LANES)
+    def combine(level_num, half, begin, end, lower_ref, upper_ref, given):
         span_rows = 2 ** (level_num - 1)
-        columns = []
-        for base in range(0, rows, LANES):
-            end = ends[base // LANES]
-            count = (end - begin) // GROUP
-            place = (lane + base) % span_rows // 16
-            static = base % span_rows // 16
-            amount = table_ref[level_num - 1][2:3, base : base + LANES]
-            reach = sublane + (amount - GROUP * place)
-            inside = reach < GROUP
-            turn = reach & (GROUP - 1)
-            steps = max(0, min(span_rows, LANES).bit_length() - 5)
-            top = end + GROUP + GROUP * (static + 2**steps - 1)
-            bottom = begin + GROUP * static
-            upper = picked[level_num - 1][bottom : min(top, given), rows + base : rows + base + LANES]
-            if top > given:
-                filler = jnp.zeros((top - given, LANES), jnp.float32)
-                upper = jnp.concatenate([upper, filler], axis=0)
-            for step in range(steps):
-                offset = GROUP * 2**step
-                flagged = (place - static) >> step & 1 == 1
-                size = upper.shape[0]
-                flagged = jnp.broadcast_to(flagged, (size - offset, LANES))
-                upper = jnp.where(flagged, upper[offset:], upper[: size - offset])
-            spun = [
-                gathered(upper[GROUP * part : GROUP * (part + 1)], turn, 0)
-                for part in range(count + 1)
-            ]
-            moved = [jnp.where(inside, spun[part], spun[part + 1]) for part in range(count)]
-            lower = picked[level_num - 1][begin:end, base : base + LANES]
-            columns.append(lower + jnp.concatenate(moved, axis=0))
-        return columns
+        base = half * half_rows
+        count = (end - begin) // GROUP
+        place = (lane + base) % span_rows // 16
+        static = base % span_rows // 16
+        amount = table_ref[level_num - 1][2:3, base : base + half_rows]
+        reach = sublane + (amount - GROUP * place)
+        inside = reach < GROUP
+        turn = reach & (GROUP - 1)
+        steps = max(0, min(span_rows, half_rows).bit_length() - 5)
+        top = end + GROUP + GROUP * (static + 2**steps - 1)
+        bottom = begin + GROUP * static
+        upper = upper_ref[bottom : min(top, given), :]
+        if top > given:
+            filler = jnp.zeros((top - given, half_rows), jnp.float32)
+            upper = jnp.concatenate([upper, filler], axis=0)
+        for step in range(steps):
+            offset = GROUP * 2**step
+            flagged = (place - static) >> step & 1 == 1
+            size = upper.shape[0]
+            flagged = jnp.broadcast_to(flagged, (size - offset, half_rows))
+            upper = jnp.where(flagged, upper[offset:], upper[: size - offset])
+        spun = [
+            gathered(upper[GROUP * part : GROUP * (part + 1)], turn, 0) for part in range(count + 1)
+        ]
+        moved = [jnp.where(inside, spun[part], spun[part + 1]) for part in range(count)]
+        return lower_ref[begin:end, :] + jnp.concatenate(moved, axis=0)
+
+    def combine_first(half, begin, end, given):
+        at = half * half_rows
+        return combine(
+            1,
+            half,
+            begin,
+            end,
+            first_picked.at[:, at : at + half_rows],
+            first_picked.at[:, rows + at : rows + at + half_rows],
+            given,
+        )
 
     loads[1].wait()
     loads[2].wait()
     ahead = ceil_16(rows + GROUP)
-    picked[0][0:ahead, :] = jnp.dot(
+    first_picked[0:ahead, :] = jnp.dot(
         own_ref[0:ahead, :], choose[...], preferred_element_type=jnp.float32
     )
-    near = combine(1, 0, rows, ahead)
     last_row = lax.broadcasted_iota(jnp.int32, (16, half_rows), 0) == 15
-    for part, values in enumerate(near):
+    for part in range(2):
+        values = combine_first(part, 0, rows, ahead)
         at = part * half_rows
         tables[0][0:rows, at : at + half_rows] = values.astype(jnp.bfloat16)
         top = (part + 1) * half_rows
         halo_out[0 : top - 16, at : at + half_rows] = values[0 : top - 16].astype(jnp.bfloat16)
-        edge = jnp.broadcast_to(picked[0][0:1, rows + at : rows + at + half_rows], (16, half_rows))
+        edge = jnp.broadcast_to(first_picked[0:1, rows + at : rows + at + half_rows], (16, half_rows))
         halo_out[top - 16 : top, at : at + half_rows] = jnp.where(
             last_row, edge, values[top - 16 : top]
         ).astype(jnp.bfloat16)
@@ -373,10 +380,11 @@
         for back in backs:
             back.start()
 
-    picked[0][ahead:window, :] = jnp.dot(
+    first_picked[ahead:window, :] = jnp.dot(
         own_ref[ahead:window, :], choose[...], preferred_element_type=jnp.float32
     )
-    for part, values in enumerate(combine(1, rows, window, window)):
+    for part in range(2):
+        values = combine_first(part, rows, window, window)
         at = part * half_rows
         tables[0][rows:window, at : at + half_rows] = values.astype(jnp.bfloat16)
 
@@ -385,33 +393,57 @@
     def prepare(level_num):
         child_rows = widest_shift(level_num)
         entries = table_ref[level_num - 1]
+        if level_num == levels:
+            choices[level_num - 2, 0] = one_hot(entries[0:1], half_rows)
+            choices[level_num - 2, 1] = one_hot(entries[1:2], half_rows)
+            return
         starts = 2 * child_rows * (lanes >> (level_num - 1))
-        choices[level_num - 2, :, 0:rows] = one_hot(starts + entries[0:1], rows)
-        choices[level_num - 2, :, rows:] = one_hot(starts + child_rows + entries[1:2], rows)
-
-    def advance(level_num, source_begin, source_end, begin, ends):
-        picked[level_num - 1][source_begin:source_end, :] = jnp.dot(
-            tables[level_num - 2][source_begin:source_end, :],
-            choices[level_num - 2],
+        lower = starts + entries[0:1]
+        upper = starts + child_rows + entries[1:2]
+        for half in range(2):
+            at = half * half_rows
+            choices[level_num - 2, half, :, 0:half_rows] = one_hot(
+                lower[:, at : at + half_rows] - at, half_rows
+            )
+            choices[level_num - 2, half, :, half_rows:] = one_hot(
+                upper[:, at : at + half_rows] - at, half_rows
+            )
+
+    def advance(level_num, half, source_begin, source_end):
+        at = half * half_rows
+        picked[level_num - 2][half, source_begin:source_end, :] = jnp.dot(
+            tables[level_num - 2][source_begin:source_end, at : at + half_rows],
+            choices[level_num - 2, half],
             preferred_element_type=jnp.float32,
         )
-        for part, values in enumerate(combine(level_num, begin, ends, source_end)):
-            at = part * half_rows
-            tables[level_num - 1][begin : begin + values.shape[0], at : at + half_rows] = (
-                values.astype(jnp.bfloat16)
-            )
-
-    valid = window - 1
-    ready = window
-    starts_late = [floor_16(valid)]
+
+    def finish(level_num, half, begin, end, given):
+        at = half * half_rows
+        lower, upper = (0, 1) if level_num == levels else (half, half)
+        low_at, high_at = (at, at) if level_num == levels else (0, half_rows)
+        tables[level_num - 1][begin:end, at : at + half_rows] = combine(
+            level_num,
+            half,
+            begin,
+            end,
+            picked[level_num - 2].at[lower, :, low_at : low_at + half_rows],
+            picked[level_num - 2].at[upper, :, high_at : high_at + half_rows],
+            given,
+        ).astype(jnp.bfloat16)
+
+    def needed(level_num, half, edge):
+        lag = 0 if half or level_num == levels else half_rows
+        return edge + still_to_come(level_num, levels) - lag
+
+    early = rows
     for level_num in range(2, levels + 1):
         prepare(level_num)
-        valid -= widest_shift(level_num)
-        end = ceil_16(valid)
-        advance(level_num, 0, ready, 0, end)
-        ready = end
-        starts_late.append(floor_16(valid))
-    early = ready
+        ends = [ceil_16(needed(level_num - 1, half, early)) for half in range(2)]
+        for half in range(2):
+            advance(level_num, half, 0, ends[half])
+        for half in range(2):
+            given = ends[1] if level_num == levels else ends[half]
+            finish(level_num, half, 0, ceil_16(needed(level_num, half, early)), given)
 
     spots = lax.broadcasted_iota(jnp.int32, (rows, rows), 0)
     shift = held.bit_length() - 1
@@ -425,41 +457,41 @@
         .astype(jnp.bfloat16)
     )
 
-    def turn_over(begin, end):
+    def turn_over(values):
         return lax.dot_general(
             placed[...],
-            tables[levels - 1][begin:end, :],
+            values,
             (((1,), (1,)), ((), ())),
             preferred_element_type=jnp.float32,
-        ).astype(jnp.bfloat16)
-
-    def spread(source, target, send_sem, recv_sem, some):
+        )
+
+    def put_blocks(target, begin):
+        blocks = turn_over(tables[levels - 1][begin : begin + rows, :]).astype(jnp.bfloat16)
+        for tile in range(rows // LANES):
+            for owner in range(owners):
+                target[owner, tile * held : (tile + 1) * held, :] = blocks[
+                    owner * held : (owner + 1) * held, tile * LANES : (tile + 1) * LANES
+                ]
+
+    def spread(source, target, size, send_sem, recv_sem):
         copies = []
         for apart in range(1, owners):
             to = lax.rem(me + apart, owners)
             copy = pltpu.make_async_remote_copy(
-                src_ref=source.at[pl.ds(pl.multiple_of(to * held, held), held)],
-                dst_ref=target.at[me],
+                src_ref=source.at[to, 0:size],
+                dst_ref=target.at[me, 0:size],
                 send_sem=send_sem.at[apart],
                 recv_sem=recv_sem.at[apart],
                 device_id={"sub": to},
                 device_id_type=MESH,
             )
-            copies.append((copy, apart))
-
-            if some:
-
-                @pl.when(me < owners - 1)
-                def _():
-                    copy.start()
-
-            else:
-                copy.start()
-        target[me] = source[pl.ds(pl.multiple_of(me * held, held), held), :]
+            copies.append(copy)
+            copy.start()
+        target[me] = source[me]
         return copies
 
-    early_out[:, 0:early] = turn_over(0, early)
-    early_copies = spread(early_out, early_in, early_send, early_recv, False)
+    put_blocks(early_out, 0)
+    early_copies = spread(early_out, early_in, 2 * held, early_send, early_recv)
 
     @pl.when(me < owners - 1)
     def _():
@@ -480,40 +512,84 @@
         late_edge = last_row & jnp.broadcast_to(amount > 0, (16, half_rows))
         fill = fill + jnp.where(late_edge, jnp.broadcast_to(edge, (16, half_rows)), 0.0)
         tables[0][window - 16 : window, at : at + half_rows] = fill.astype(jnp.bfloat16)
-    ready = window + rows
     for level_num in range(2, levels + 1):
-        end = ceil_16(window + still_to_come(level_num, levels))
-        ends = [end if level_num == levels else ceil_16(end - half_rows), end]
-        advance(
-            level_num, starts_late[level_num - 2], ready, starts_late[level_num - 1], ends
-        )
-        ready = end
-    late_out[...] = turn_over(early, window)
-    late_copies = spread(late_out, late_in, late_send, late_recv, True)
+        begins = [floor_16(needed(level_num - 1, half, early)) for half in range(2)]
+        ends = [ceil_16(needed(level_num - 1, half, window)) for half in range(2)]
+        for half in range(2):
+            advance(level_num, half, begins[half], ends[half])
+        for half in range(2):
+            given = ends[1] if level_num == levels else ends[half]
+            finish(
+                level_num,
+                half,
+                floor_16(needed(level_num, half, early)),
+                ceil_16(needed(level_num, half, window)),
+                given,
+            )
+    put_blocks(late_out, early)
+    rest = window - 2 * rows
+    tail = tables[levels - 1][2 * rows : window, :]
+    tail = turn_over(jnp.concatenate([tail] * (LANES // rest), axis=0))
+    row_spot = lax.broadcasted_iota(jnp.int32, (rows, LANES), 0)
+    turned = window * me // rest % (LANES // rest)
+    lane_spot = lax.broadcasted_iota(jnp.int32, (rows, LANES), 1) // rest
+    tail = jnp.where((row_spot + lane_spot) % (LANES // rest) == turned, tail, 0.0).astype(jnp.bfloat16)
+    packed_rows = rows * rest // LANES
+    gather_rows = (
+        lax.broadcasted_iota(jnp.int32, (packed_rows, rows), 1) // (LANES // rest)
+        == lax.broadcasted_iota(jnp.int32, (packed_rows, rows), 0)
+    )
+    tail = jnp.dot(
+        gather_rows.astype(jnp.float32).astype(jnp.bfloat16),
+        tail,
+        preferred_element_type=jnp.float32,
+    ).astype(jnp.bfloat16)
+    extra = packed_rows // owners
+    for owner in range(owners):
+        late_out[owner, 2 * held : 2 * held + extra, :] = tail[
+            owner * extra : (owner + 1) * extra
+        ]
+    late_copies = spread(late_out, late_in, 2 * held + extra, late_send, late_recv)
 
     wide_lane = lax.broadcasted_iota(jnp.int32, (held, LANES), 1)
     pieces = [[] for _ in range(fold_size)]
     for source in range(owners):
-        for late, begin, end in ((False, 0, early), (True, early, window)):
-            for at in range(begin, end, LANES):
-                fold, part = divmod(window * source + at, LANES)
-                count = min(LANES, end - at)
-                for where, low, high in (
-                    (fold, part, min(LANES, part + count)),
-                    (fold + 1, 0, part + count - LANES),
-                ):
-                    if where < fold_size and low < high:
-                        pieces[where].append((low, high, source, late, at - begin, part))
+        for at in range(0, window, LANES):
+            fold, part = divmod(window * source + at, LANES)
+            count = min(LANES, window - at)
+            for where, low, high in (
+                (fold, part, min(LANES, part + count)),
+                (fold + 1, 0, part + count - LANES),
+            ):
+                if where < fold_size and low < high:
+                    pieces[where].append((low, high, source, at >= early, at, part))
     rolled = {}
 
     def rolled_tile(source, late, at, part):
-        if (source, late, at) not in rolled:
-            value = (late_in if late else early_in)[source, :, at : at + LANES]
-            value = value.astype(jnp.float32)
-            if part:
-                value = pltpu.roll(value, part, axis=1)
-            rolled[source, late, at] = value
-        return rolled[source, late, at]
+        if (source, at) not in rolled:
+            if at < 2 * rows:
+                place = (at - early if late else at) // LANES * held
+                value = (late_in if late else early_in)[source, place : place + held, :]
+                value = value.astype(jnp.float32)
+                if part:
+                    value = pltpu.roll(value, part, axis=1)
+            else:
+                value = late_in[source, 2 * held : 3 * held, :].astype(jnp.float32)
+                value = jnp.concatenate(
+                    [
+                        pltpu.roll(
+                            jnp.broadcast_to(value[row : row + 1], (LANES // rest, LANES)),
+                            0,
+                            axis=1,
+                            stride=rest,
+                            stride_axis=0,
+                        )
+                        for row in range(extra)
+                    ],
+                    axis=0,
+                )
+            rolled[source, at] = value
+        return rolled[source, at]
 
     def assemble(which):
         for fold in range(fold_size):
@@ -536,20 +612,13 @@
                     value = jnp.where((wide_lane >= low) & (wide_lane < high), piece, value)
             folded[where, :] = value
 
-    for copy, apart in early_copies:
+    for copy in early_copies:
         copy.wait()
     assemble(False)
     for load in loads[3:]:
         load.wait()
-    for copy, apart in late_copies:
-
-        @pl.when(me < owners - 1)
-        def _():
-            copy.wait_send()
-
-        @pl.when(lax.rem(me + owners - apart, owners) < owners - 1)
-        def _():
-            copy.wait_recv()
+    for copy in late_copies:
+        copy.wait()
 
     assemble(True)
 
@@ -609,7 +678,6 @@
     held = rows // owners
     length = owners * (window - held)
     fold_size = length // LANES
-    early = window - rows
     whole = window + rows
     order = channel_order.reshape(1, channels)
     first_table, twist, third_table = transform_tables(fold_size, length)
@@ -627,15 +695,16 @@
             pltpu.VMEM(third_table.shape, jnp.bfloat16),
             pltpu.VMEM((channels, channels), jnp.bfloat16),
             pltpu.VMEM((channels, channels), jnp.bfloat16),
-            pltpu.VMEM((levels - 1, rows, 2 * rows), jnp.bfloat16),
-            [pltpu.VMEM((whole, 2 * rows), jnp.float32)] * levels,
+            pltpu.VMEM((levels - 1, 2, rows // 2, rows), jnp.bfloat16),
+            pltpu.VMEM((window, channels), jnp.float32),
+            [pltpu.VMEM((2, whole, rows), jnp.float32)] * (levels - 1),
             [pltpu.VMEM((whole, rows), jnp.bfloat16)] * levels,
             pltpu.VMEM((rows, rows), jnp.bfloat16),
             pltpu.VMEM((rows, rows), jnp.bfloat16),
-            pltpu.VMEM((rows, -(-early // LANES) * LANES), jnp.bfloat16),
-            pltpu.VMEM((rows, rows), jnp.bfloat16),
-            pltpu.VMEM((owners, held, -(-early // LANES) * LANES), jnp.bfloat16),
-            pltpu.VMEM((owners, held, rows), jnp.bfloat16),
+            pltpu.VMEM((owners, 2 * held, LANES), jnp.bfloat16),
+            pltpu.VMEM((owners, 3 * held, LANES), jnp.bfloat16),
+            pltpu.VMEM((owners, 2 * held, LANES), jnp.bfloat16),
+            pltpu.VMEM((owners, 3 * held, LANES), jnp.bfloat16),
             pltpu.VMEM((FOLD_PITCH * fold_size, LANES), jnp.float32),
             pltpu.VMEM((held * fold_size, 2 * LANES), jnp.bfloat16),
             pltpu.VMEM((POWER_PITCH * held, LANES), jnp.float32),
@@ -663,7 +732,8 @@
         and channels == 2 * rows
         and rows == 2 ** (levels - 1)
         and length == 64 * LANES
-        and window > 2 * rows
+        and window == 2 * rows + 16
+        and owners == 16
     )
 
 

time: 17.8 us -> 16.8 us (0.944)
  Pallas kernels: 16.9 us -> 15.9 us
    pallas_call x1, Pallas kernels: 16.9 us -> 15.9 us  [local_sliced(): pl.pallas_call(functools.partial(merge_kernel, owners, length), out_shape...]
where the time goes in v4:
time: 16.8 us; the launch traced here: 16.6 us
  Pallas kernels  15.9 us (95%)
  local copies, waits for them, and re-layouts  0.71 us (4%)
    pallas_call x1, Pallas kernels, local_sliced(): pl.pallas_call(functools.partial(merge_kernel, owners, length), out_shape...  15.9 us
    unnamed x1, local copies, waits for them, and re-layouts  0.71 us

profile of v4, /device:TPU:0, one launch (start us, length us, event | category | flops | bytes accessed | tf_op | source)
XLA Modules:
  0.0 16.6 jit_solution(1723047628916933281)
XLA Ops:
  0.0 15.9 %merge_rows.1 = f32[16,4096]{1,0:T(8,128)S(1)} custom-call(s32[1,512]{1,0:T(1,128)} %bitcast.1, s32[9,3,256]{2,1,0:T(4,128)} %table_hbm.1, bf16[528,512]{1,0:T(8,128)(2,1)} %own_hbm.1, bf16[128,64]{1,0:T(8,128)(2,1)} %constant.6.clone.first_hbm, f32[2,64,128]{2,1,0:T(8,128)} %constant.7.clone.twist_hbm, bf16[128,256]{1,0:T(8,128)(2,1)} %constant.8.clone.third_hbm), custom_call_target="tpu_custom_call" | custom-call | tf_op jit(solution)/shard_map/merge_rows/pallas_call | solution.py:684
  15.9 0.7 %copy.8 = f32[16,4096]{1,0:T(8,128)} copy(f32[16,4096]{1,0:T(8,128)S(1)} %merge_rows.1) | data formatting | bytes 524288

commit v5 on v4

--- a/solution.py
+++ b/solution.py
@@ -345,49 +345,6 @@
         )
 
     loads[1].wait()
-    loads[2].wait()
-    ahead = ceil_16(rows + GROUP)
-    first_picked[0:ahead, :] = jnp.dot(
-        own_ref[0:ahead, :], choose[...], preferred_element_type=jnp.float32
-    )
-    last_row = lax.broadcasted_iota(jnp.int32, (16, half_rows), 0) == 15
-    for part in range(2):
-        values = combine_first(part, 0, rows, ahead)
-        at = part * half_rows
-        tables[0][0:rows, at : at + half_rows] = values.astype(jnp.bfloat16)
-        top = (part + 1) * half_rows
-        halo_out[0 : top - 16, at : at + half_rows] = values[0 : top - 16].astype(jnp.bfloat16)
-        edge = jnp.broadcast_to(first_picked[0:1, rows + at : rows + at + half_rows], (16, half_rows))
-        halo_out[top - 16 : top, at : at + half_rows] = jnp.where(
-            last_row, edge, values[top - 16 : top]
-        ).astype(jnp.bfloat16)
-
-    pl.semaphore_wait(barrier, owners - 1)
-    backs = [
-        pltpu.make_async_remote_copy(
-            src_ref=halo_out.at[0:count, first : first + half_rows],
-            dst_ref=tables[0].at[window : window + count, first : first + half_rows],
-            send_sem=halo_sem.at[part],
-            recv_sem=halo_sem.at[2 + part],
-            device_id={"sub": lax.rem(me + owners - 1, owners)},
-            device_id_type=MESH,
-        )
-        for part, (count, first) in enumerate(((rows, half_rows), (half_rows, 0)))
-    ]
-
-    @pl.when(me > 0)
-    def _():
-        for back in backs:
-            back.start()
-
-    first_picked[ahead:window, :] = jnp.dot(
-        own_ref[ahead:window, :], choose[...], preferred_element_type=jnp.float32
-    )
-    for part in range(2):
-        values = combine_first(part, rows, window, window)
-        at = part * half_rows
-        tables[0][rows:window, at : at + half_rows] = values.astype(jnp.bfloat16)
-
     lanes = lax.broadcasted_iota(jnp.int32, (1, rows), 1)
 
     def prepare(level_num):
@@ -409,6 +366,34 @@
                 upper[:, at : at + half_rows] - at, half_rows
             )
 
+    for level_num in range(2, levels + 1):
+        prepare(level_num)
+
+    loads[2].wait()
+    ahead = ceil_16(rows + GROUP)
+    first_picked[0:ahead, :] = jnp.dot(
+        own_ref[0:ahead, :], choose[...], preferred_element_type=jnp.float32
+    )
+    last_row = lax.broadcasted_iota(jnp.int32, (16, half_rows), 0) == 15
+    for part in range(2):
+        values = combine_first(part, 0, rows, ahead)
+        at = part * half_rows
+        tables[0][0:rows, at : at + half_rows] = values.astype(jnp.bfloat16)
+        top = (part + 1) * half_rows
+        halo_out[0 : top - 16, at : at + half_rows] = values[0 : top - 16].astype(jnp.bfloat16)
+        edge = jnp.broadcast_to(first_picked[0:1, rows + at : rows + at + half_rows], (16, half_rows))
+        halo_out[top - 16 : top, at : at + half_rows] = jnp.where(
+            last_row, edge, values[top - 16 : top]
+        ).astype(jnp.bfloat16)
+
+    first_picked[ahead:window, :] = jnp.dot(
+        own_ref[ahead:window, :], choose[...], preferred_element_type=jnp.float32
+    )
+    for part in range(2):
+        values = combine_first(part, rows, window, window)
+        at = part * half_rows
+        tables[0][rows:window, at : at + half_rows] = values.astype(jnp.bfloat16)
+
     def advance(level_num, half, source_begin, source_end):
         at = half * half_rows
         picked[level_num - 2][half, source_begin:source_end, :] = jnp.dot(
@@ -436,8 +421,25 @@
         return edge + still_to_come(level_num, levels) - lag
 
     early = rows
-    for level_num in range(2, levels + 1):
-        prepare(level_num)
+    pl.semaphore_wait(barrier, owners - 1)
+    backs = [
+        pltpu.make_async_remote_copy(
+            src_ref=halo_out.at[0:count, first : first + half_rows],
+            dst_ref=tables[0].at[window : window + count, first : first + half_rows],
+            send_sem=halo_sem.at[part],
+            recv_sem=halo_sem.at[2 + part],
+            device_id={"sub": lax.rem(me + owners - 1, owners)},
+            device_id_type=MESH,
+        )
+        for part, (count, first) in enumerate(((rows, half_rows), (half_rows, 0)))
+    ]
+
+    @pl.when(me > 0)
+    def _():
+        for back in backs:
+            back.start()
+
+    for level_num in range(1 + 1, levels + 1):
         ends = [ceil_16(needed(level_num - 1, half, early)) for half in range(2)]
         for half in range(2):
             advance(level_num, half, 0, ends[half])

time: 16.8 us -> 16 us (0.952)
  Pallas kernels: 15.9 us -> 15.1 us
    pallas_call x1, Pallas kernels: 15.9 us -> 15.1 us  [local_sliced(): pl.pallas_call(functools.partial(merge_kernel, owners, length), out_shape...]
where the time goes in v5:
time: 16 us; the launch traced here: 15.8 us
  Pallas kernels  15.1 us (94%)
  local copies, waits for them, and re-layouts  0.71 us (4%)
    pallas_call x1, Pallas kernels, local_sliced(): pl.pallas_call(functools.partial(merge_kernel, owners, length), out_shape...  15.1 us
    unnamed x1, local copies, waits for them, and re-layouts  0.71 us

profile of v5, /device:TPU:0, one launch (start us, length us, event | category | flops | bytes accessed | tf_op | source)
XLA Modules:
  0.0 15.8 jit_solution(6910413339783005362)
XLA Ops:
  0.0 15.1 %merge_rows.1 = f32[16,4096]{1,0:T(8,128)S(1)} custom-call(s32[1,512]{1,0:T(1,128)} %bitcast.1, s32[9,3,256]{2,1,0:T(4,128)} %table_hbm.1, bf16[528,512]{1,0:T(8,128)(2,1)} %own_hbm.1, bf16[128,64]{1,0:T(8,128)(2,1)} %constant.6.clone.first_hbm, f32[2,64,128]{2,1,0:T(8,128)} %constant.7.clone.twist_hbm, bf16[128,256]{1,0:T(8,128)(2,1)} %constant.8.clone.third_hbm), custom_call_target="tpu_custom_call" | custom-call | tf_op jit(solution)/shard_map/merge_rows/pallas_call | solution.py:686
  15.1 0.7 %copy.8 = f32[16,4096]{1,0:T(8,128)} copy(f32[16,4096]{1,0:T(8,128)S(1)} %merge_rows.1) | data formatting | bytes 524288

commit v6 on v5

--- a/solution.py
+++ b/solution.py
@@ -244,10 +244,7 @@
     twisted,
     powers,
     halo_sem,
-    early_send,
-    early_recv,
-    late_send,
-    late_recv,
+    exchange_sem,
     load_sem,
 ):
     levels, _, rows = table_ref.shape
@@ -278,10 +275,11 @@
     stripe = channels // owners
     for apart in range(owners):
         if apart:
+            far = owners // 2 + (apart // 2 if apart % 2 else -(apart // 2))
             pl.semaphore_signal(
                 barrier,
                 inc=1,
-                device_id={"sub": lax.rem(me + apart, owners)},
+                device_id={"sub": lax.rem(me + far, owners)},
                 device_id_type=MESH,
             )
         split[apart * stripe : (apart + 1) * stripe, :] = one_hot(paired - apart * stripe, stripe)
@@ -439,7 +437,7 @@
         for back in backs:
             back.start()
 
-    for level_num in range(1 + 1, levels + 1):
+    for level_num in range(2, levels + 1):
         ends = [ceil_16(needed(level_num - 1, half, early)) for half in range(2)]
         for half in range(2):
             advance(level_num, half, 0, ends[half])
@@ -476,24 +474,28 @@
                 ]
 
     def spread(source, target, size, send_sem, recv_sem):
-        copies = []
         for apart in range(1, owners):
             to = lax.rem(me + apart, owners)
-            copy = pltpu.make_async_remote_copy(
+            pltpu.make_async_remote_copy(
                 src_ref=source.at[to, 0:size],
                 dst_ref=target.at[me, 0:size],
-                send_sem=send_sem.at[apart],
-                recv_sem=recv_sem.at[apart],
+                send_sem=send_sem,
+                recv_sem=recv_sem,
                 device_id={"sub": to},
                 device_id_type=MESH,
-            )
-            copies.append(copy)
-            copy.start()
+            ).start()
         target[me] = source[me]
-        return copies
+        return pltpu.make_async_remote_copy(
+            src_ref=source.at[1:owners, 0:size],
+            dst_ref=target.at[1:owners, 0:size],
+            send_sem=send_sem,
+            recv_sem=recv_sem,
+            device_id={"sub": lax.rem(me + 1, owners)},
+            device_id_type=MESH,
+        )
 
     put_blocks(early_out, 0)
-    early_copies = spread(early_out, early_in, 2 * held, early_send, early_recv)
+    early_blocks = spread(early_out, early_in, 2 * held, exchange_sem.at[0], exchange_sem.at[1])
 
     @pl.when(me < owners - 1)
     def _():
@@ -551,7 +553,7 @@
         late_out[owner, 2 * held : 2 * held + extra, :] = tail[
             owner * extra : (owner + 1) * extra
         ]
-    late_copies = spread(late_out, late_in, 2 * held + extra, late_send, late_recv)
+    late_blocks = spread(late_out, late_in, 2 * held + extra, exchange_sem.at[2], exchange_sem.at[3])
 
     wide_lane = lax.broadcasted_iota(jnp.int32, (held, LANES), 1)
     pieces = [[] for _ in range(fold_size)]
@@ -614,13 +616,13 @@
                     value = jnp.where((wide_lane >= low) & (wide_lane < high), piece, value)
             folded[where, :] = value
 
-    for copy in early_copies:
-        copy.wait()
+    early_blocks.wait_recv()
     assemble(False)
     for load in loads[3:]:
         load.wait()
-    for copy in late_copies:
-        copy.wait()
+    early_blocks.wait_send()
+    late_blocks.wait_send()
+    late_blocks.wait_recv()
 
     assemble(True)
 
@@ -711,10 +713,7 @@
             pltpu.VMEM((held * fold_size, 2 * LANES), jnp.bfloat16),
             pltpu.VMEM((POWER_PITCH * held, LANES), jnp.float32),
             pltpu.SemaphoreType.DMA((4,)),
-            pltpu.SemaphoreType.DMA((owners,)),
-            pltpu.SemaphoreType.DMA((owners,)),
-            pltpu.SemaphoreType.DMA((owners,)),
-            pltpu.SemaphoreType.DMA((owners,)),
+            pltpu.SemaphoreType.DMA((4,)),
             pltpu.SemaphoreType.DMA((6,)),
         ],
         compiler_params=pltpu.CompilerParams(

time: 16 us -> 15.4 us (0.963)
  Pallas kernels: 15.1 us -> 14.5 us
    pallas_call x1, Pallas kernels: 15.1 us -> 14.5 us  [local_sliced(): pl.pallas_call(functools.partial(merge_kernel, owners, length), out_shape...]
where the time goes in v6:
time: 15.4 us; the launch traced here: 15.2 us
  Pallas kernels  14.5 us (94%)
  local copies, waits for them, and re-layouts  0.71 us (5%)
    pallas_call x1, Pallas kernels, local_sliced(): pl.pallas_call(functools.partial(merge_kernel, owners, length), out_shape...  14.5 us
    unnamed x1, local copies, waits for them, and re-layouts  0.71 us

profile of v6, /device:TPU:0, one launch (start us, length us, event | category | flops | bytes accessed | tf_op | source)
XLA Modules:
  0.0 15.2 jit_solution(5393904998535213797)
XLA Ops:
  0.0 14.5 %merge_rows.1 = f32[16,4096]{1,0:T(8,128)S(1)} custom-call(s32[1,512]{1,0:T(1,128)} %bitcast.1, s32[9,3,256]{2,1,0:T(4,128)} %table_hbm.1, bf16[528,512]{1,0:T(8,128)(2,1)} %own_hbm.1, bf16[128,64]{1,0:T(8,128)(2,1)} %constant.6.clone.first_hbm, f32[2,64,128]{2,1,0:T(8,128)} %constant.7.clone.twist_hbm, bf16[128,256]{1,0:T(8,128)(2,1)} %constant.8.clone.third_hbm), custom_call_target="tpu_custom_call" | custom-call | tf_op jit(solution)/shard_map/merge_rows/pallas_call | solution.py:688
  14.5 0.7 %copy.8 = f32[16,4096]{1,0:T(8,128)} copy(f32[16,4096]{1,0:T(8,128)S(1)} %merge_rows.1) | data formatting | bytes 524288

commit v7 on v6

--- a/solution.py
+++ b/solution.py
@@ -202,6 +202,33 @@
 def one_hot(row_index, depth):
     rows = lax.broadcasted_iota(jnp.int32, (depth, row_index.shape[1]), 0)
     return (rows == row_index).astype(jnp.float32).astype(jnp.bfloat16)
+
+
+def one_hot_fast(row_index, depth):
+    count = row_index.shape[1]
+    stripes = []
+    for base in range(0, depth, 2 * LANES):
+        size = min(2 * LANES, depth - base)
+        rows = lax.broadcasted_iota(jnp.int32, (size, LANES), 0).astype(jnp.float32)
+        rows = rows.astype(jnp.bfloat16)
+        wanted = jnp.broadcast_to((row_index - base).astype(jnp.float32), (16, count))
+        wanted = wanted.astype(jnp.bfloat16)
+        one, zero = jnp.ones((size, LANES), jnp.bfloat16), jnp.zeros((size, LANES), jnp.bfloat16)
+        stripes.append(
+            jnp.concatenate(
+                [
+                    jnp.where(
+                        rows
+                        == jnp.concatenate([wanted[:, at : at + LANES]] * (size // 16), axis=0),
+                        one,
+                        zero,
+                    )
+                    for at in range(0, count, LANES)
+                ],
+                axis=1,
+            )
+        )
+    return stripes[0] if len(stripes) == 1 else jnp.concatenate(stripes, axis=0)
 
 
 def floor_16(count):
@@ -282,7 +309,7 @@
                 device_id={"sub": lax.rem(me + far, owners)},
                 device_id_type=MESH,
             )
-        split[apart * stripe : (apart + 1) * stripe, :] = one_hot(paired - apart * stripe, stripe)
+        split[apart * stripe : (apart + 1) * stripe, :] = one_hot_fast(paired - apart * stripe, stripe)
     half_rows = rows // 2
 
     @pl.when(me == owners - 1)
@@ -296,7 +323,7 @@
     digits = jnp.dot(
         digits.astype(jnp.bfloat16), split[...], preferred_element_type=jnp.float32
     ).astype(jnp.int32)
-    choose[...] = one_hot(digits[0:1] * 64 + digits[1:2], channels)
+    choose[...] = one_hot_fast(digits[0:1] * 64 + digits[1:2], channels)
 
     lane = lax.broadcasted_iota(jnp.int32, (1, LANES), 1)
     sublane = lax.broadcasted_iota(jnp.int32, (GROUP, LANES), 0)
@@ -620,8 +647,6 @@
     assemble(False)
     for load in loads[3:]:
         load.wait()
-    early_blocks.wait_send()
-    late_blocks.wait_send()
     late_blocks.wait_recv()
 
     assemble(True)
@@ -669,6 +694,8 @@
             out_ref[block : block + GROUP, tile * LANES : (tile + 1) * LANES] = powers[
                 pl.ds(block * POWER_PITCH + tile, GROUP, stride=POWER_PITCH), :
             ]
+    early_blocks.wait_send()
+    late_blocks.wait_send()
 
 
 def in_place(*operands):

time: 15.4 us -> 15.4 us (level)
  no operation moved by 1% of the time
where the time goes in v7:
time: 15.4 us; the launch traced here: 15.2 us
  Pallas kernels  14.4 us (94%)
  local copies, waits for them, and re-layouts  0.71 us (5%)
    pallas_call x1, Pallas kernels, local_sliced(): pl.pallas_call(functools.partial(merge_kernel, owners, length), out_shape...  14.4 us
    unnamed x1, local copies, waits for them, and re-layouts  0.71 us

profile of v7, /device:TPU:0, one launch (start us, length us, event | category | flops | bytes accessed | tf_op | source)
XLA Modules:
  0.0 15.2 jit_solution(8116351715143946150)
XLA Ops:
  0.0 14.4 %merge_rows.1 = f32[16,4096]{1,0:T(8,128)S(1)} custom-call(s32[1,512]{1,0:T(1,128)} %bitcast.1, s32[9,3,256]{2,1,0:T(4,128)} %table_hbm.1, bf16[528,512]{1,0:T(8,128)(2,1)} %own_hbm.1, bf16[128,64]{1,0:T(8,128)(2,1)} %constant.6.clone.first_hbm, f32[2,64,128]{2,1,0:T(8,128)} %constant.7.clone.twist_hbm, bf16[128,256]{1,0:T(8,128)(2,1)} %constant.8.clone.third_hbm), custom_call_target="tpu_custom_call" | custom-call | tf_op jit(solution)/shard_map/merge_rows/pallas_call | solution.py:715
  14.5 0.7 %copy.8 = f32[16,4096]{1,0:T(8,128)} copy(f32[16,4096]{1,0:T(8,128)S(1)} %merge_rows.1) | data formatting | bytes 524288

commit v8 on v6

--- a/solution.py
+++ b/solution.py
@@ -429,7 +429,7 @@
             device_id={"sub": lax.rem(me + owners - 1, owners)},
             device_id_type=MESH,
         )
-        for part, (count, first) in enumerate(((rows, half_rows), (half_rows, 0)))
+        for part, (count, first) in enumerate(((half_rows, 0), (rows, half_rows)))
     ]
 
     @pl.when(me > 0)

time: 15.4 us -> 15.4 us (level)
  no operation moved by 1% of the time
where the time goes in v8:
time: 15.4 us; the launch traced here: 15.2 us
  Pallas kernels  14.5 us (94%)
  local copies, waits for them, and re-layouts  0.71 us (5%)
    pallas_call x1, Pallas kernels, local_sliced(): pl.pallas_call(functools.partial(merge_kernel, owners, length), out_shape...  14.5 us
    unnamed x1, local copies, waits for them, and re-layouts  0.71 us

profile of v8, /device:TPU:0, one launch (start us, length us, event | category | flops | bytes accessed | tf_op | source)
XLA Modules:
  0.0 15.2 jit_solution(3025151856944731467)
XLA Ops:
  0.0 14.5 %merge_rows.1 = f32[16,4096]{1,0:T(8,128)S(1)} custom-call(s32[1,512]{1,0:T(1,128)} %bitcast.1, s32[9,3,256]{2,1,0:T(4,128)} %table_hbm.1, bf16[528,512]{1,0:T(8,128)(2,1)} %own_hbm.1, bf16[128,64]{1,0:T(8,128)(2,1)} %constant.6.clone.first_hbm, f32[2,64,128]{2,1,0:T(8,128)} %constant.7.clone.twist_hbm, bf16[128,256]{1,0:T(8,128)(2,1)} %constant.8.clone.third_hbm), custom_call_target="tpu_custom_call" | custom-call | tf_op jit(solution)/shard_map/merge_rows/pallas_call | solution.py:688
  14.5 0.7 %copy.8 = f32[16,4096]{1,0:T(8,128)} copy(f32[16,4096]{1,0:T(8,128)S(1)} %merge_rows.1) | data formatting | bytes 524288
